TPU v7x, 256 devices: a whole 4x4x8 slice. The times are simulated.
256 devices in a mesh: ctx: 32 (over y_lo, z, core), tp: 8 (over x, y_hi).
Axes of the slice: x: 4, y: 4 (y_hi: 2, y_lo: 2; y = y_hi * 2 + y_lo), z: 8, core: 2. Of those that a mesh axis runs over, the one named last changes fastest.
Arguments:
- queries: bfloat16 [16384, 4096], P('ctx', 'tp'), may hold values from -5 to 5
- keys: bfloat16 [16384, 4096], P('ctx', 'tp'), may hold values from -5 to 5
- values: bfloat16 [16384, 4096], P('ctx', 'tp'), may hold values from -21 to 21
- log_decay: float32 [32, 16384], P('tp', 'ctx'), may hold values from -0.7 to 0
- gate: bfloat16 [16384, 4096], P('ctx', 'tp'), may hold values from -6 to 6
- gain: float32 [4096], P('tp'), may hold values from 0.5 to 1.5
- grad_out: bfloat16 [16384, 4096], P(('ctx', 'tp')), may hold values from -20 to 20
Outputs:
- query_grad: bfloat16 [16384, 4096], P('ctx', 'tp')
- key_grad: bfloat16 [16384, 4096], P('ctx', 'tp')
- value_grad: bfloat16 [16384, 4096], P('ctx', 'tp')
- gate_grad: bfloat16 [16384, 4096], P('ctx', 'tp')
- gain_grad: float32 [4096], P('tp')
All inputs are finite; a program needn't handle non-finite values.
Results may differ from a plain program's by a relative error of at most 0.005.
Values may be sent and summed in bfloat16 or wider, within the bound.
A program may use at most 64 MiB of HBM per device.

v0:
```python
import jax
import jax.numpy as jnp
from jax import lax
from jax.sharding import PartitionSpec as P

HEAD = 128
BLOCK = 512


HIGH_PRECISION = lax.Precision.HIGHEST
EPSILON = 1e-06


def passed_along(value, axis, steps):
    count = lax.axis_size(axis)
    leading, last = (max(0, -steps), min(count, count - steps))
    return lax.ppermute(value, axis, [(source, source + steps) for source in range(leading, last)])


def state_sweep(block_decay_rates, partial_terms, reverse_order):

    def step_forward_fn(carried_state, element):
        rate_row, addend = element
        return (jnp.exp(rate_row)[:, None, None] * carried_state + addend, carried_state)

    final, before = lax.scan(
        step_forward_fn,
        jnp.zeros_like(partial_terms[0]),
        (block_decay_rates, partial_terms),
        reverse=reverse_order,
    )
    return (before, final)


def local(queries, keys, values, log_decay, gate, gain, grad_out):
    rows_here, cols_here = queries.shape
    heads_here = cols_here // HEAD
    count = rows_here // BLOCK
    channels = cols_here * lax.axis_size("tp")
    grad_rows = lax.all_to_all(grad_out, "tp", split_axis=1, concat_axis=0, tiled=True)
    shape4 = (count, BLOCK, heads_here, HEAD)
    query_blocks = queries.reshape(shape4)
    key_blocks = keys.reshape(shape4)
    value_blocks = values.reshape(shape4)
    decay_sum = jnp.cumsum(log_decay.reshape(heads_here, count, BLOCK), axis=2)
    by_head = jnp.transpose(decay_sum, (1, 0, 2))
    decay_sum = jnp.transpose(decay_sum, (1, 2, 0))
    block_decay_rate = decay_sum[:, -1, :]
    causal = jnp.tril(jnp.ones((BLOCK, BLOCK), dtype=bool))
    spread = by_head[:, :, :, None] - by_head[:, :, None, :]
    table = jnp.where(causal[None, None], jnp.exp(jnp.minimum(spread, 0.0)), 0.0)
    attention_scores = jnp.einsum(
        "blhd,bmhd->bhlm", query_blocks, key_blocks, preferred_element_type=jnp.float32
    )
    probs = (attention_scores * table).astype(jnp.bfloat16)
    intra = jnp.einsum("bhlm,bmhe->blhe", probs, value_blocks, preferred_element_type=jnp.float32)
    growth = jnp.exp(decay_sum)[..., None]
    decay_shrink = jnp.exp(block_decay_rate[:, None, :] - decay_sum)[..., None]
    full_value_rows = value_blocks.astype(jnp.float32)
    query_decayed = query_blocks.astype(jnp.float32) * growth
    key_with_decay = key_blocks.astype(jnp.float32) * decay_shrink
    partial_terms = jnp.einsum(
        "zoas,zoai->zasi", key_with_decay, full_value_rows, precision=HIGH_PRECISION
    )
    state_before_block, block_local_state = state_sweep(block_decay_rate, partial_terms, False)
    totals = jnp.cumsum(block_decay_rate, axis=0)
    device_decay = jnp.exp(totals[-1])

    def forward_turn(turn_number, carried_state):
        return passed_along(
            device_decay[:, None, None] * carried_state + block_local_state, "ctx", 1
        )

    incoming = lax.fori_loop(
        0, lax.axis_size("ctx") - 1, forward_turn, jnp.zeros_like(block_local_state)
    )
    entering = jnp.exp(totals - block_decay_rate)
    prev_states = state_before_block + entering[:, :, None, None] * incoming[None]
    attention = intra + jnp.einsum(
        "blhd,bhde->blhe", query_decayed, prev_states, precision=HIGH_PRECISION
    )
    gain_heads = gain.reshape(heads_here, HEAD)
    grad_blocks = grad_rows.reshape(shape4).astype(jnp.float32)
    opened = jax.nn.sigmoid(gate.reshape(shape4).astype(jnp.float32))
    dnorm = grad_blocks * opened
    dscaled = dnorm * gain_heads
    squares = jnp.sum(attention * attention, axis=(2, 3))
    inner = jnp.sum(attention * dscaled, axis=(2, 3))
    squares, inner = lax.psum((squares, inner), "tp")
    rscale = lax.rsqrt(squares / channels + EPSILON)[:, :, None, None]
    normed = attention * rscale * gain_heads
    gate_grad = (
        (grad_blocks * normed * opened * (1.0 - opened))
        .astype(jnp.bfloat16)
        .reshape(rows_here, cols_here)
    )
    gain_part = jnp.sum(dnorm * attention * rscale, axis=(0, 1)).reshape(cols_here)
    gain_grad = lax.psum(gain_part, "ctx")
    dattn = (
        dscaled * rscale - attention * (inner[:, :, None, None] * rscale**3 / channels)
    ).astype(jnp.bfloat16)
    dprobs = jnp.einsum("blhe,bmhe->bhlm", dattn, value_blocks, preferred_element_type=jnp.float32)
    scores_gradient = (dprobs * table).astype(jnp.bfloat16)
    wide_dattn = dattn.astype(jnp.float32)
    query_grad = jnp.einsum(
        "bhlm,bmhd->blhd", scores_gradient, key_blocks, preferred_element_type=jnp.float32
    )
    query_grad = query_grad + jnp.einsum(
        "blhe,bhde->blhd", wide_dattn * growth, prev_states, precision=HIGH_PRECISION
    )
    backterms = jnp.einsum("zoas,zoai->zasi", query_decayed, wide_dattn, precision=HIGH_PRECISION)
    after_local, local_grad = state_sweep(block_decay_rate, backterms, True)

    def backward_turn(turn_number, carried_state):
        return passed_along(device_decay[:, None, None] * carried_state + local_grad, "ctx", -1)

    outgoing = lax.fori_loop(0, lax.axis_size("ctx") - 1, backward_turn, jnp.zeros_like(local_grad))
    leaving = jnp.exp(totals[-1][None, :] - totals)
    after_states = after_local + leaving[:, :, None, None] * outgoing[None]
    key_grad = jnp.einsum(
        "bhlm,blhd->bmhd", scores_gradient, query_blocks, preferred_element_type=jnp.float32
    )
    key_grad = key_grad + jnp.einsum(
        "bmhe,bhde->bmhd", full_value_rows * decay_shrink, after_states, precision=HIGH_PRECISION
    )
    value_grad = jnp.einsum("bhlm,blhe->bmhe", probs, dattn, preferred_element_type=jnp.float32)
    value_grad = value_grad + jnp.einsum(
        "bmhd,bhde->bmhe", key_with_decay, after_states, precision=HIGH_PRECISION
    )
    flat = (rows_here, cols_here)
    return (
        query_grad.astype(jnp.bfloat16).reshape(flat),
        key_grad.astype(jnp.bfloat16).reshape(flat),
        value_grad.astype(jnp.bfloat16).reshape(flat),
        gate_grad,
        gain_grad,
    )


def solution(mesh):
    return jax.shard_map(
        local,
        mesh=mesh,
        in_specs=(
            P("ctx", "tp"),
            P("ctx", "tp"),
            P("ctx", "tp"),
            P("tp", "ctx"),
            P("ctx", "tp"),
            P("tp"),
            P(("ctx", "tp"), None),
        ),
        out_specs=(P("ctx", "tp"), P("ctx", "tp"), P("ctx", "tp"), P("ctx", "tp"), P("tp")),
        check_vma=False,
    )
```

profile of v0, /device:TPU:24, one launch (start us, length us, event | category | flops | bytes accessed | tf_op | source)
XLA Modules:
  0.0 765.0 jit_solution(1937952808525632403)
XLA Ops:
  19.0 308.1 %while.4 = (s32[]{:T(128)}, f32[4,128,128]{2,1,0:T(8,128)S(1)}, f32[4]{0:T(128)S(1)}, f32[4,128,128]{2,1,0:T(8,128)S(1)}, s32[]{:T(128)}) while((s32[]{:T(128)}, f32[4,128,128]{2,1,0:T(8,128)S(1)}, f32[4]{0:T(128)S(1)}, f32[4,128,128]{2,1,0:T(8,128)S(1)}, s32[]{:T(128)}) %tuple.47), condition=%wide.region_3.4_spmd, body=%wide.region_2.3_spmd.sunk | while | flops 131074 | bytes 1835125 | solution.py:74
  21.0 8.9 %collective-permute-done = f32[4,128,128]{2,1,0:T(8,128)S(1)} collective-permute-done((f32[4,128,128]{2,1,0:T(8,128)S(1)}, f32[4,128,128]{2,1,0:T(8,128)S(1)}, u32[]{:S(2)}, u32[]{:S(2)}) %collective-permute-start) | collective-permute-done | bytes 262176 | tf_op jit(solution)/shard_map/while/body/eval_jaxpr/ppermute | solution.py:17
  32.0 7.9 %collective-permute-done = f32[4,128,128]{2,1,0:T(8,128)S(1)} collective-permute-done((f32[4,128,128]{2,1,0:T(8,128)S(1)}, f32[4,128,128]{2,1,0:T(8,128)S(1)}, u32[]{:S(2)}, u32[]{:S(2)}) %collective-permute-start) | collective-permute-done | bytes 262176 | tf_op jit(solution)/shard_map/while/body/eval_jaxpr/ppermute | solution.py:17
  41.9 7.9 %collective-permute-done = f32[4,128,128]{2,1,0:T(8,128)S(1)} collective-permute-done((f32[4,128,128]{2,1,0:T(8,128)S(1)}, f32[4,128,128]{2,1,0:T(8,128)S(1)}, u32[]{:S(2)}, u32[]{:S(2)}) %collective-permute-start) | collective-permute-done | bytes 262176 | tf_op jit(solution)/shard_map/while/body/eval_jaxpr/ppermute | solution.py:17
  51.8 7.9 %collective-permute-done = f32[4,128,128]{2,1,0:T(8,128)S(1)} collective-permute-done((f32[4,128,128]{2,1,0:T(8,128)S(1)}, f32[4,128,128]{2,1,0:T(8,128)S(1)}, u32[]{:S(2)}, u32[]{:S(2)}) %collective-permute-start) | collective-permute-done | bytes 262176 | tf_op jit(solution)/shard_map/while/body/eval_jaxpr/ppermute | solution.py:17
  61.7 7.9 %collective-permute-done = f32[4,128,128]{2,1,0:T(8,128)S(1)} collective-permute-done((f32[4,128,128]{2,1,0:T(8,128)S(1)}, f32[4,128,128]{2,1,0:T(8,128)S(1)}, u32[]{:S(2)}, u32[]{:S(2)}) %collective-permute-start) | collective-permute-done | bytes 262176 | tf_op jit(solution)/shard_map/while/body/eval_jaxpr/ppermute | solution.py:17
  71.5 7.9 %collective-permute-done = f32[4,128,128]{2,1,0:T(8,128)S(1)} collective-permute-done((f32[4,128,128]{2,1,0:T(8,128)S(1)}, f32[4,128,128]{2,1,0:T(8,128)S(1)}, u32[]{:S(2)}, u32[]{:S(2)}) %collective-permute-start) | collective-permute-done | bytes 262176 | tf_op jit(solution)/shard_map/while/body/eval_jaxpr/ppermute | solution.py:17
  81.4 7.9 %collective-permute-done = f32[4,128,128]{2,1,0:T(8,128)S(1)} collective-permute-done((f32[4,128,128]{2,1,0:T(8,128)S(1)}, f32[4,128,128]{2,1,0:T(8,128)S(1)}, u32[]{:S(2)}, u32[]{:S(2)}) %collective-permute-start) | collective-permute-done | bytes 262176 | tf_op jit(solution)/shard_map/while/body/eval_jaxpr/ppermute | solution.py:17
  91.3 7.9 %collective-permute-done = f32[4,128,128]{2,1,0:T(8,128)S(1)} collective-permute-done((f32[4,128,128]{2,1,0:T(8,128)S(1)}, f32[4,128,128]{2,1,0:T(8,128)S(1)}, u32[]{:S(2)}, u32[]{:S(2)}) %collective-permute-start) | collective-permute-done | bytes 262176 | tf_op jit(solution)/shard_map/while/body/eval_jaxpr/ppermute | solution.py:17
  101.2 7.9 %collective-permute-done = f32[4,128,128]{2,1,0:T(8,128)S(1)} collective-permute-done((f32[4,128,128]{2,1,0:T(8,128)S(1)}, f32[4,128,128]{2,1,0:T(8,128)S(1)}, u32[]{:S(2)}, u32[]{:S(2)}) %collective-permute-start) | collective-permute-done | bytes 262176 | tf_op jit(solution)/shard_map/while/body/eval_jaxpr/ppermute | solution.py:17
  111.1 7.9 %collective-permute-done = f32[4,128,128]{2,1,0:T(8,128)S(1)} collective-permute-done((f32[4,128,128]{2,1,0:T(8,128)S(1)}, f32[4,128,128]{2,1,0:T(8,128)S(1)}, u32[]{:S(2)}, u32[]{:S(2)}) %collective-permute-start) | collective-permute-done | bytes 262176 | tf_op jit(solution)/shard_map/while/body/eval_jaxpr/ppermute | solution.py:17
  121.0 7.9 %collective-permute-done = f32[4,128,128]{2,1,0:T(8,128)S(1)} collective-permute-done((f32[4,128,128]{2,1,0:T(8,128)S(1)}, f32[4,128,128]{2,1,0:T(8,128)S(1)}, u32[]{:S(2)}, u32[]{:S(2)}) %collective-permute-start) | collective-permute-done | bytes 262176 | tf_op jit(solution)/shard_map/while/body/eval_jaxpr/ppermute | solution.py:17
  130.9 7.9 %collective-permute-done = f32[4,128,128]{2,1,0:T(8,128)S(1)} collective-permute-done((f32[4,128,128]{2,1,0:T(8,128)S(1)}, f32[4,128,128]{2,1,0:T(8,128)S(1)}, u32[]{:S(2)}, u32[]{:S(2)}) %collective-permute-start) | collective-permute-done | bytes 262176 | tf_op jit(solution)/shard_map/while/body/eval_jaxpr/ppermute | solution.py:17
  140.8 7.9 %collective-permute-done = f32[4,128,128]{2,1,0:T(8,128)S(1)} collective-permute-done((f32[4,128,128]{2,1,0:T(8,128)S(1)}, f32[4,128,128]{2,1,0:T(8,128)S(1)}, u32[]{:S(2)}, u32[]{:S(2)}) %collective-permute-start) | collective-permute-done | bytes 262176 | tf_op jit(solution)/shard_map/while/body/eval_jaxpr/ppermute | solution.py:17
  150.7 7.9 %collective-permute-done = f32[4,128,128]{2,1,0:T(8,128)S(1)} collective-permute-done((f32[4,128,128]{2,1,0:T(8,128)S(1)}, f32[4,128,128]{2,1,0:T(8,128)S(1)}, u32[]{:S(2)}, u32[]{:S(2)}) %collective-permute-start) | collective-permute-done | bytes 262176 | tf_op jit(solution)/shard_map/while/body/eval_jaxpr/ppermute | solution.py:17
  160.6 7.9 %collective-permute-done = f32[4,128,128]{2,1,0:T(8,128)S(1)} collective-permute-done((f32[4,128,128]{2,1,0:T(8,128)S(1)}, f32[4,128,128]{2,1,0:T(8,128)S(1)}, u32[]{:S(2)}, u32[]{:S(2)}) %collective-permute-start) | collective-permute-done | bytes 262176 | tf_op jit(solution)/shard_map/while/body/eval_jaxpr/ppermute | solution.py:17
  170.5 7.9 %collective-permute-done = f32[4,128,128]{2,1,0:T(8,128)S(1)} collective-permute-done((f32[4,128,128]{2,1,0:T(8,128)S(1)}, f32[4,128,128]{2,1,0:T(8,128)S(1)}, u32[]{:S(2)}, u32[]{:S(2)}) %collective-permute-start) | collective-permute-done | bytes 262176 | tf_op jit(solution)/shard_map/while/body/eval_jaxpr/ppermute | solution.py:17
  180.4 7.9 %collective-permute-done = f32[4,128,128]{2,1,0:T(8,128)S(1)} collective-permute-done((f32[4,128,128]{2,1,0:T(8,128)S(1)}, f32[4,128,128]{2,1,0:T(8,128)S(1)}, u32[]{:S(2)}, u32[]{:S(2)}) %collective-permute-start) | collective-permute-done | bytes 262176 | tf_op jit(solution)/shard_map/while/body/eval_jaxpr/ppermute | solution.py:17
  190.3 7.9 %collective-permute-done = f32[4,128,128]{2,1,0:T(8,128)S(1)} collective-permute-done((f32[4,128,128]{2,1,0:T(8,128)S(1)}, f32[4,128,128]{2,1,0:T(8,128)S(1)}, u32[]{:S(2)}, u32[]{:S(2)}) %collective-permute-start) | collective-permute-done | bytes 262176 | tf_op jit(solution)/shard_map/while/body/eval_jaxpr/ppermute | solution.py:17
  200.2 7.9 %collective-permute-done = f32[4,128,128]{2,1,0:T(8,128)S(1)} collective-permute-done((f32[4,128,128]{2,1,0:T(8,128)S(1)}, f32[4,128,128]{2,1,0:T(8,128)S(1)}, u32[]{:S(2)}, u32[]{:S(2)}) %collective-permute-start) | collective-permute-done | bytes 262176 | tf_op jit(solution)/shard_map/while/body/eval_jaxpr/ppermute | solution.py:17
  210.1 7.9 %collective-permute-done = f32[4,128,128]{2,1,0:T(8,128)S(1)} collective-permute-done((f32[4,128,128]{2,1,0:T(8,128)S(1)}, f32[4,128,128]{2,1,0:T(8,128)S(1)}, u32[]{:S(2)}, u32[]{:S(2)}) %collective-permute-start) | collective-permute-done | bytes 262176 | tf_op jit(solution)/shard_map/while/body/eval_jaxpr/ppermute | solution.py:17
  220.0 7.9 %collective-permute-done = f32[4,128,128]{2,1,0:T(8,128)S(1)} collective-permute-done((f32[4,128,128]{2,1,0:T(8,128)S(1)}, f32[4,128,128]{2,1,0:T(8,128)S(1)}, u32[]{:S(2)}, u32[]{:S(2)}) %collective-permute-start) | collective-permute-done | bytes 262176 | tf_op jit(solution)/shard_map/while/body/eval_jaxpr/ppermute | solution.py:17
  229.9 7.9 %collective-permute-done = f32[4,128,128]{2,1,0:T(8,128)S(1)} collective-permute-done((f32[4,128,128]{2,1,0:T(8,128)S(1)}, f32[4,128,128]{2,1,0:T(8,128)S(1)}, u32[]{:S(2)}, u32[]{:S(2)}) %collective-permute-start) | collective-permute-done | bytes 262176 | tf_op jit(solution)/shard_map/while/body/eval_jaxpr/ppermute | solution.py:17
  239.8 7.9 %collective-permute-done = f32[4,128,128]{2,1,0:T(8,128)S(1)} collective-permute-done((f32[4,128,128]{2,1,0:T(8,128)S(1)}, f32[4,128,128]{2,1,0:T(8,128)S(1)}, u32[]{:S(2)}, u32[]{:S(2)}) %collective-permute-start) | collective-permute-done | bytes 262176 | tf_op jit(solution)/shard_map/while/body/eval_jaxpr/ppermute | solution.py:17
  249.7 7.9 %collective-permute-done = f32[4,128,128]{2,1,0:T(8,128)S(1)} collective-permute-done((f32[4,128,128]{2,1,0:T(8,128)S(1)}, f32[4,128,128]{2,1,0:T(8,128)S(1)}, u32[]{:S(2)}, u32[]{:S(2)}) %collective-permute-start) | collective-permute-done | bytes 262176 | tf_op jit(solution)/shard_map/while/body/eval_jaxpr/ppermute | solution.py:17
  279.4 8.0 %collective-permute-done = f32[4,128,128]{2,1,0:T(8,128)S(1)} collective-permute-done((f32[4,128,128]{2,1,0:T(8,128)S(1)}, f32[4,128,128]{2,1,0:T(8,128)S(1)}, u32[]{:S(2)}, u32[]{:S(2)}) %collective-permute-start) | collective-permute-done | bytes 262176 | tf_op jit(solution)/shard_map/while/body/eval_jaxpr/ppermute | solution.py:17
  289.4 7.9 %collective-permute-done = f32[4,128,128]{2,1,0:T(8,128)S(1)} collective-permute-done((f32[4,128,128]{2,1,0:T(8,128)S(1)}, f32[4,128,128]{2,1,0:T(8,128)S(1)}, u32[]{:S(2)}, u32[]{:S(2)}) %collective-permute-start) | collective-permute-done | bytes 262176 | tf_op jit(solution)/shard_map/while/body/eval_jaxpr/ppermute | solution.py:17
  309.2 7.9 %collective-permute-done = f32[4,128,128]{2,1,0:T(8,128)S(1)} collective-permute-done((f32[4,128,128]{2,1,0:T(8,128)S(1)}, f32[4,128,128]{2,1,0:T(8,128)S(1)}, u32[]{:S(2)}, u32[]{:S(2)}) %collective-permute-start) | collective-permute-done | bytes 262176 | tf_op jit(solution)/shard_map/while/body/eval_jaxpr/ppermute | solution.py:17
  330.4 20.3 %psum.21 = f32[1,512]{1,0:T(1,128)S(1)} all-reduce(f32[1,512]{1,0:T(1,128)S(1)} %bitcast.172), channel_id=1, replica_groups=mesh['ctx'=32,'tp'=8] {'tp'}, use_global_device_ids=true, to_apply=%region_5.6 | all-reduce | flops 512 | bytes 4096 | tf_op jit(solution)/shard_map/psum | solution.py:89
  357.3 23.8 %psum.22 = f32[512]{0:T(512)S(1)} all-reduce(f32[512]{0:T(512)S(1)} %get-tuple-element.92), channel_id=1, replica_groups=mesh['ctx'=32,'tp'=8] {'tp'}, use_global_device_ids=true, to_apply=%region_7.8 | all-reduce | flops 512 | bytes 4096 | tf_op jit(solution)/shard_map/psum | solution.py:89
  388.7 302.8 %while.5 = (s32[]{:T(128)}, f32[4,128,128]{2,1,0:T(8,128)S(1)}, f32[4]{0:T(128)S(1)}, f32[4,128,128]{2,1,0:T(8,128)S(1)}, s32[]{:T(128)}) while((s32[]{:T(128)}, f32[4,128,128]{2,1,0:T(8,128)S(1)}, f32[4]{0:T(128)S(1)}, f32[4,128,128]{2,1,0:T(8,128)S(1)}, s32[]{:T(128)}) %tuple.53), condition=%wide.region_9.10_spmd, body=%wide.region_8.9_spmd.sunk | while | flops 131074 | bytes 1835125 | solution.py:117
  707.4 57.5 %psum.23 = f32[512]{0:T(512)} all-reduce(f32[512]{0:T(512)S(1)} %bitcast.170), channel_id=1, replica_groups=mesh['ctx'=32,'tp'=8] {'ctx'}, use_global_device_ids=true, to_apply=%region_11.12 | all-reduce | flops 512 | bytes 4096 | tf_op jit(solution)/shard_map/psum | solution.py:98
  (235 shorter events, 447.8 us)
Async XLA Ops:
  2.6 348.1 %all-to-all-start = ((bf16[64,8,512]{2,0,1:T(8,128)(2,1)}), bf16[64,8,512]{2,0,1:T(8,128)(2,1)}, u32[]{:S(2)}, u32[]{:S(2)}) async-start(bf16[64,8,512]{2,0,1:T(8,128)(2,1)} %bitcast.147), calls=%async_computation | async-start | bytes 1048576 | tf_op jit(solution)/shard_map/all_to_all | solution.py:40
  19.1 10.9 %collective-permute-start = (f32[4,128,128]{2,1,0:T(8,128)S(1)}, f32[4,128,128]{2,1,0:T(8,128)S(1)}, u32[]{:S(2)}, u32[]{:S(2)}) collective-permute-start(f32[4,128,128]{2,1,0:T(8,128)S(1)} %multiply_add_fusion.4), channel_id=1, source_target_pairs={{0,8},{8,16},{16,24},{24,32},{32,40},{40,48},{48,56},{56,64},{64,7... | collective-permute-start | bytes 786440 | tf_op jit(solution)/shard_map/while/body/eval_jaxpr/ppermute | solution.py:17
  277.4 9.9 %collective-permute-start = (f32[4,128,128]{2,1,0:T(8,128)S(1)}, f32[4,128,128]{2,1,0:T(8,128)S(1)}, u32[]{:S(2)}, u32[]{:S(2)}) collective-permute-start(f32[4,128,128]{2,1,0:T(8,128)S(1)} %multiply_add_fusion.4), channel_id=1, source_target_pairs={{0,8},{8,16},{16,24},{24,32},{32,40},{40,48},{48,56},{56,64},{64,7... | collective-permute-start | bytes 786440 | tf_op jit(solution)/shard_map/while/body/eval_jaxpr/ppermute | solution.py:17
  287.4 9.8 %collective-permute-start = (f32[4,128,128]{2,1,0:T(8,128)S(1)}, f32[4,128,128]{2,1,0:T(8,128)S(1)}, u32[]{:S(2)}, u32[]{:S(2)}) collective-permute-start(f32[4,128,128]{2,1,0:T(8,128)S(1)} %multiply_add_fusion.4), channel_id=1, source_target_pairs={{0,8},{8,16},{16,24},{24,32},{32,40},{40,48},{48,56},{56,64},{64,7... | collective-permute-start | bytes 786440 | tf_op jit(solution)/shard_map/while/body/eval_jaxpr/ppermute | solution.py:17
  307.3 9.9 %collective-permute-start = (f32[4,128,128]{2,1,0:T(8,128)S(1)}, f32[4,128,128]{2,1,0:T(8,128)S(1)}, u32[]{:S(2)}, u32[]{:S(2)}) collective-permute-start(f32[4,128,128]{2,1,0:T(8,128)S(1)} %multiply_add_fusion.4), channel_id=1, source_target_pairs={{0,8},{8,16},{16,24},{24,32},{32,40},{40,48},{48,56},{56,64},{64,7... | collective-permute-start | bytes 786440 | tf_op jit(solution)/shard_map/while/body/eval_jaxpr/ppermute | solution.py:17
  394.7 9.8 %collective-permute-start.1 = (f32[4,128,128]{2,1,0:T(8,128)S(1)}, f32[4,128,128]{2,1,0:T(8,128)S(1)}, u32[]{:S(2)}, u32[]{:S(2)}) collective-permute-start(f32[4,128,128]{2,1,0:T(8,128)S(1)} %multiply_add_fusion.5), channel_id=1, source_target_pairs={{8,0},{16,8},{24,16},{32,24},{40,32},{48,40},{56,48},{64,56},{72,6... | collective-permute-start | bytes 786440 | tf_op jit(solution)/shard_map/while/body/eval_jaxpr/ppermute | solution.py:17
  404.6 9.8 %collective-permute-start.1 = (f32[4,128,128]{2,1,0:T(8,128)S(1)}, f32[4,128,128]{2,1,0:T(8,128)S(1)}, u32[]{:S(2)}, u32[]{:S(2)}) collective-permute-start(f32[4,128,128]{2,1,0:T(8,128)S(1)} %multiply_add_fusion.5), channel_id=1, source_target_pairs={{8,0},{16,8},{24,16},{32,24},{40,32},{48,40},{56,48},{64,56},{72,6... | collective-permute-start | bytes 786440 | tf_op jit(solution)/shard_map/while/body/eval_jaxpr/ppermute | solution.py:17
  414.5 9.8 %collective-permute-start.1 = (f32[4,128,128]{2,1,0:T(8,128)S(1)}, f32[4,128,128]{2,1,0:T(8,128)S(1)}, u32[]{:S(2)}, u32[]{:S(2)}) collective-permute-start(f32[4,128,128]{2,1,0:T(8,128)S(1)} %multiply_add_fusion.5), channel_id=1, source_target_pairs={{8,0},{16,8},{24,16},{32,24},{40,32},{48,40},{56,48},{64,56},{72,6... | collective-permute-start | bytes 786440 | tf_op jit(solution)/shard_map/while/body/eval_jaxpr/ppermute | solution.py:17
  424.4 9.8 %collective-permute-start.1 = (f32[4,128,128]{2,1,0:T(8,128)S(1)}, f32[4,128,128]{2,1,0:T(8,128)S(1)}, u32[]{:S(2)}, u32[]{:S(2)}) collective-permute-start(f32[4,128,128]{2,1,0:T(8,128)S(1)} %multiply_add_fusion.5), channel_id=1, source_target_pairs={{8,0},{16,8},{24,16},{32,24},{40,32},{48,40},{56,48},{64,56},{72,6... | collective-permute-start | bytes 786440 | tf_op jit(solution)/shard_map/while/body/eval_jaxpr/ppermute | solution.py:17
  434.3 9.8 %collective-permute-start.1 = (f32[4,128,128]{2,1,0:T(8,128)S(1)}, f32[4,128,128]{2,1,0:T(8,128)S(1)}, u32[]{:S(2)}, u32[]{:S(2)}) collective-permute-start(f32[4,128,128]{2,1,0:T(8,128)S(1)} %multiply_add_fusion.5), channel_id=1, source_target_pairs={{8,0},{16,8},{24,16},{32,24},{40,32},{48,40},{56,48},{64,56},{72,6... | collective-permute-start | bytes 786440 | tf_op jit(solution)/shard_map/while/body/eval_jaxpr/ppermute | solution.py:17
  444.2 9.8 %collective-permute-start.1 = (f32[4,128,128]{2,1,0:T(8,128)S(1)}, f32[4,128,128]{2,1,0:T(8,128)S(1)}, u32[]{:S(2)}, u32[]{:S(2)}) collective-permute-start(f32[4,128,128]{2,1,0:T(8,128)S(1)} %multiply_add_fusion.5), channel_id=1, source_target_pairs={{8,0},{16,8},{24,16},{32,24},{40,32},{48,40},{56,48},{64,56},{72,6... | collective-permute-start | bytes 786440 | tf_op jit(solution)/shard_map/while/body/eval_jaxpr/ppermute | solution.py:17
  454.1 9.8 %collective-permute-start.1 = (f32[4,128,128]{2,1,0:T(8,128)S(1)}, f32[4,128,128]{2,1,0:T(8,128)S(1)}, u32[]{:S(2)}, u32[]{:S(2)}) collective-permute-start(f32[4,128,128]{2,1,0:T(8,128)S(1)} %multiply_add_fusion.5), channel_id=1, source_target_pairs={{8,0},{16,8},{24,16},{32,24},{40,32},{48,40},{56,48},{64,56},{72,6... | collective-permute-start | bytes 786440 | tf_op jit(solution)/shard_map/while/body/eval_jaxpr/ppermute | solution.py:17
  464.0 9.8 %collective-permute-start.1 = (f32[4,128,128]{2,1,0:T(8,128)S(1)}, f32[4,128,128]{2,1,0:T(8,128)S(1)}, u32[]{:S(2)}, u32[]{:S(2)}) collective-permute-start(f32[4,128,128]{2,1,0:T(8,128)S(1)} %multiply_add_fusion.5), channel_id=1, source_target_pairs={{8,0},{16,8},{24,16},{32,24},{40,32},{48,40},{56,48},{64,56},{72,6... | collective-permute-start | bytes 786440 | tf_op jit(solution)/shard_map/while/body/eval_jaxpr/ppermute | solution.py:17
  473.9 9.8 %collective-permute-start.1 = (f32[4,128,128]{2,1,0:T(8,128)S(1)}, f32[4,128,128]{2,1,0:T(8,128)S(1)}, u32[]{:S(2)}, u32[]{:S(2)}) collective-permute-start(f32[4,128,128]{2,1,0:T(8,128)S(1)} %multiply_add_fusion.5), channel_id=1, source_target_pairs={{8,0},{16,8},{24,16},{32,24},{40,32},{48,40},{56,48},{64,56},{72,6... | collective-permute-start | bytes 786440 | tf_op jit(solution)/shard_map/while/body/eval_jaxpr/ppermute | solution.py:17
  483.7 9.8 %collective-permute-start.1 = (f32[4,128,128]{2,1,0:T(8,128)S(1)}, f32[4,128,128]{2,1,0:T(8,128)S(1)}, u32[]{:S(2)}, u32[]{:S(2)}) collective-permute-start(f32[4,128,128]{2,1,0:T(8,128)S(1)} %multiply_add_fusion.5), channel_id=1, source_target_pairs={{8,0},{16,8},{24,16},{32,24},{40,32},{48,40},{56,48},{64,56},{72,6... | collective-permute-start | bytes 786440 | tf_op jit(solution)/shard_map/while/body/eval_jaxpr/ppermute | solution.py:17
  493.6 9.8 %collective-permute-start.1 = (f32[4,128,128]{2,1,0:T(8,128)S(1)}, f32[4,128,128]{2,1,0:T(8,128)S(1)}, u32[]{:S(2)}, u32[]{:S(2)}) collective-permute-start(f32[4,128,128]{2,1,0:T(8,128)S(1)} %multiply_add_fusion.5), channel_id=1, source_target_pairs={{8,0},{16,8},{24,16},{32,24},{40,32},{48,40},{56,48},{64,56},{72,6... | collective-permute-start | bytes 786440 | tf_op jit(solution)/shard_map/while/body/eval_jaxpr/ppermute | solution.py:17
  503.5 9.8 %collective-permute-start.1 = (f32[4,128,128]{2,1,0:T(8,128)S(1)}, f32[4,128,128]{2,1,0:T(8,128)S(1)}, u32[]{:S(2)}, u32[]{:S(2)}) collective-permute-start(f32[4,128,128]{2,1,0:T(8,128)S(1)} %multiply_add_fusion.5), channel_id=1, source_target_pairs={{8,0},{16,8},{24,16},{32,24},{40,32},{48,40},{56,48},{64,56},{72,6... | collective-permute-start | bytes 786440 | tf_op jit(solution)/shard_map/while/body/eval_jaxpr/ppermute | solution.py:17
  513.4 9.8 %collective-permute-start.1 = (f32[4,128,128]{2,1,0:T(8,128)S(1)}, f32[4,128,128]{2,1,0:T(8,128)S(1)}, u32[]{:S(2)}, u32[]{:S(2)}) collective-permute-start(f32[4,128,128]{2,1,0:T(8,128)S(1)} %multiply_add_fusion.5), channel_id=1, source_target_pairs={{8,0},{16,8},{24,16},{32,24},{40,32},{48,40},{56,48},{64,56},{72,6... | collective-permute-start | bytes 786440 | tf_op jit(solution)/shard_map/while/body/eval_jaxpr/ppermute | solution.py:17
  523.3 9.8 %collective-permute-start.1 = (f32[4,128,128]{2,1,0:T(8,128)S(1)}, f32[4,128,128]{2,1,0:T(8,128)S(1)}, u32[]{:S(2)}, u32[]{:S(2)}) collective-permute-start(f32[4,128,128]{2,1,0:T(8,128)S(1)} %multiply_add_fusion.5), channel_id=1, source_target_pairs={{8,0},{16,8},{24,16},{32,24},{40,32},{48,40},{56,48},{64,56},{72,6... | collective-permute-start | bytes 786440 | tf_op jit(solution)/shard_map/while/body/eval_jaxpr/ppermute | solution.py:17
  533.2 9.8 %collective-permute-start.1 = (f32[4,128,128]{2,1,0:T(8,128)S(1)}, f32[4,128,128]{2,1,0:T(8,128)S(1)}, u32[]{:S(2)}, u32[]{:S(2)}) collective-permute-start(f32[4,128,128]{2,1,0:T(8,128)S(1)} %multiply_add_fusion.5), channel_id=1, source_target_pairs={{8,0},{16,8},{24,16},{32,24},{40,32},{48,40},{56,48},{64,56},{72,6... | collective-permute-start | bytes 786440 | tf_op jit(solution)/shard_map/while/body/eval_jaxpr/ppermute | solution.py:17
  543.1 9.8 %collective-permute-start.1 = (f32[4,128,128]{2,1,0:T(8,128)S(1)}, f32[4,128,128]{2,1,0:T(8,128)S(1)}, u32[]{:S(2)}, u32[]{:S(2)}) collective-permute-start(f32[4,128,128]{2,1,0:T(8,128)S(1)} %multiply_add_fusion.5), channel_id=1, source_target_pairs={{8,0},{16,8},{24,16},{32,24},{40,32},{48,40},{56,48},{64,56},{72,6... | collective-permute-start | bytes 786440 | tf_op jit(solution)/shard_map/while/body/eval_jaxpr/ppermute | solution.py:17
  553.0 9.8 %collective-permute-start.1 = (f32[4,128,128]{2,1,0:T(8,128)S(1)}, f32[4,128,128]{2,1,0:T(8,128)S(1)}, u32[]{:S(2)}, u32[]{:S(2)}) collective-permute-start(f32[4,128,128]{2,1,0:T(8,128)S(1)} %multiply_add_fusion.5), channel_id=1, source_target_pairs={{8,0},{16,8},{24,16},{32,24},{40,32},{48,40},{56,48},{64,56},{72,6... | collective-permute-start | bytes 786440 | tf_op jit(solution)/shard_map/while/body/eval_jaxpr/ppermute | solution.py:17
  562.9 9.8 %collective-permute-start.1 = (f32[4,128,128]{2,1,0:T(8,128)S(1)}, f32[4,128,128]{2,1,0:T(8,128)S(1)}, u32[]{:S(2)}, u32[]{:S(2)}) collective-permute-start(f32[4,128,128]{2,1,0:T(8,128)S(1)} %multiply_add_fusion.5), channel_id=1, source_target_pairs={{8,0},{16,8},{24,16},{32,24},{40,32},{48,40},{56,48},{64,56},{72,6... | collective-permute-start | bytes 786440 | tf_op jit(solution)/shard_map/while/body/eval_jaxpr/ppermute | solution.py:17
  572.8 9.8 %collective-permute-start.1 = (f32[4,128,128]{2,1,0:T(8,128)S(1)}, f32[4,128,128]{2,1,0:T(8,128)S(1)}, u32[]{:S(2)}, u32[]{:S(2)}) collective-permute-start(f32[4,128,128]{2,1,0:T(8,128)S(1)} %multiply_add_fusion.5), channel_id=1, source_target_pairs={{8,0},{16,8},{24,16},{32,24},{40,32},{48,40},{56,48},{64,56},{72,6... | collective-permute-start | bytes 786440 | tf_op jit(solution)/shard_map/while/body/eval_jaxpr/ppermute | solution.py:17
  582.7 9.8 %collective-permute-start.1 = (f32[4,128,128]{2,1,0:T(8,128)S(1)}, f32[4,128,128]{2,1,0:T(8,128)S(1)}, u32[]{:S(2)}, u32[]{:S(2)}) collective-permute-start(f32[4,128,128]{2,1,0:T(8,128)S(1)} %multiply_add_fusion.5), channel_id=1, source_target_pairs={{8,0},{16,8},{24,16},{32,24},{40,32},{48,40},{56,48},{64,56},{72,6... | collective-permute-start | bytes 786440 | tf_op jit(solution)/shard_map/while/body/eval_jaxpr/ppermute | solution.py:17
  592.6 9.8 %collective-permute-start.1 = (f32[4,128,128]{2,1,0:T(8,128)S(1)}, f32[4,128,128]{2,1,0:T(8,128)S(1)}, u32[]{:S(2)}, u32[]{:S(2)}) collective-permute-start(f32[4,128,128]{2,1,0:T(8,128)S(1)} %multiply_add_fusion.5), channel_id=1, source_target_pairs={{8,0},{16,8},{24,16},{32,24},{40,32},{48,40},{56,48},{64,56},{72,6... | collective-permute-start | bytes 786440 | tf_op jit(solution)/shard_map/while/body/eval_jaxpr/ppermute | solution.py:17
  612.4 9.8 %collective-permute-start.1 = (f32[4,128,128]{2,1,0:T(8,128)S(1)}, f32[4,128,128]{2,1,0:T(8,128)S(1)}, u32[]{:S(2)}, u32[]{:S(2)}) collective-permute-start(f32[4,128,128]{2,1,0:T(8,128)S(1)} %multiply_add_fusion.5), channel_id=1, source_target_pairs={{8,0},{16,8},{24,16},{32,24},{40,32},{48,40},{56,48},{64,56},{72,6... | collective-permute-start | bytes 786440 | tf_op jit(solution)/shard_map/while/body/eval_jaxpr/ppermute | solution.py:17
  622.3 9.8 %collective-permute-start.1 = (f32[4,128,128]{2,1,0:T(8,128)S(1)}, f32[4,128,128]{2,1,0:T(8,128)S(1)}, u32[]{:S(2)}, u32[]{:S(2)}) collective-permute-start(f32[4,128,128]{2,1,0:T(8,128)S(1)} %multiply_add_fusion.5), channel_id=1, source_target_pairs={{8,0},{16,8},{24,16},{32,24},{40,32},{48,40},{56,48},{64,56},{72,6... | collective-permute-start | bytes 786440 | tf_op jit(solution)/shard_map/while/body/eval_jaxpr/ppermute | solution.py:17
  632.2 9.8 %collective-permute-start.1 = (f32[4,128,128]{2,1,0:T(8,128)S(1)}, f32[4,128,128]{2,1,0:T(8,128)S(1)}, u32[]{:S(2)}, u32[]{:S(2)}) collective-permute-start(f32[4,128,128]{2,1,0:T(8,128)S(1)} %multiply_add_fusion.5), channel_id=1, source_target_pairs={{8,0},{16,8},{24,16},{32,24},{40,32},{48,40},{56,48},{64,56},{72,6... | collective-permute-start | bytes 786440 | tf_op jit(solution)/shard_map/while/body/eval_jaxpr/ppermute | solution.py:17
  661.9 9.8 %collective-permute-start.1 = (f32[4,128,128]{2,1,0:T(8,128)S(1)}, f32[4,128,128]{2,1,0:T(8,128)S(1)}, u32[]{:S(2)}, u32[]{:S(2)}) collective-permute-start(f32[4,128,128]{2,1,0:T(8,128)S(1)} %multiply_add_fusion.5), channel_id=1, source_target_pairs={{8,0},{16,8},{24,16},{32,24},{40,32},{48,40},{56,48},{64,56},{72,6... | collective-permute-start | bytes 786440 | tf_op jit(solution)/shard_map/while/body/eval_jaxpr/ppermute | solution.py:17
  671.8 9.8 %collective-permute-start.1 = (f32[4,128,128]{2,1,0:T(8,128)S(1)}, f32[4,128,128]{2,1,0:T(8,128)S(1)}, u32[]{:S(2)}, u32[]{:S(2)}) collective-permute-start(f32[4,128,128]{2,1,0:T(8,128)S(1)} %multiply_add_fusion.5), channel_id=1, source_target_pairs={{8,0},{16,8},{24,16},{32,24},{40,32},{48,40},{56,48},{64,56},{72,6... | collective-permute-start | bytes 786440 | tf_op jit(solution)/shard_map/while/body/eval_jaxpr/ppermute | solution.py:17
  681.7 9.8 %collective-permute-start.1 = (f32[4,128,128]{2,1,0:T(8,128)S(1)}, f32[4,128,128]{2,1,0:T(8,128)S(1)}, u32[]{:S(2)}, u32[]{:S(2)}) collective-permute-start(f32[4,128,128]{2,1,0:T(8,128)S(1)} %multiply_add_fusion.5), channel_id=1, source_target_pairs={{8,0},{16,8},{24,16},{32,24},{40,32},{48,40},{56,48},{64,56},{72,6... | collective-permute-start | bytes 786440 | tf_op jit(solution)/shard_map/while/body/eval_jaxpr/ppermute | solution.py:17
  (45 other events, 364.2 us)
where the time goes:
time: 768 us; the launch traced here: 765 us
  waiting for transfers between devices  365 us (48%)
  starting transfers between devices  247 us (32%)
  blocking collectives  102 us (13%)
  matrix products  22.4 us (3%)
  local copies, waits for them, and re-layouts  13.8 us (2%)
  other arithmetic  13.7 us (2%)
    ppermute x62, waiting for transfers between devices, passed_along(): lax.ppermute(value, axis, [(source, source + steps) for source in range(l...  365 us
    ppermute x62, starting transfers between devices, passed_along(): lax.ppermute(value, axis, [(source, source + steps) for source in range(l...  239 us
    psum x1, blocking collectives, local(): gain_grad = lax.psum(gain_part, 'ctx')  57.5 us
    psum x2, blocking collectives, local(): squares, inner = lax.psum((squares, inner), 'tp')  44 us
  transfers between devices with their start and end apart: 63, of which 62 were waited for; matrix products, arithmetic and copies ran while one was open for 2% of the time, Pallas kernels for 0%

commit v1 on v0

v1 whole, which is shorter than its diff:
```python
import functools

import jax
import jax.numpy as jnp
from jax import lax
from jax.experimental import pallas as pl
from jax.experimental.pallas import tpu as pltpu
from jax.sharding import PartitionSpec as P

HEAD = 128
BLOCK = 512
CHUNK = 128
CHUNKS = BLOCK // CHUNK
EPSILON = 1e-06
MESH = pl.DeviceIdType.MESH
F32, BF16 = jnp.float32, jnp.bfloat16

DECAY, GRAD, STATE_UP, STATE_DOWN, NORM, BACK_UP, BACK_DOWN, GAIN = range(8)


def dot(a, b, over_a, over_b):
    return lax.dot_general(
        a, b, (((over_a,), (over_b,)), ((), ())), preferred_element_type=F32
    )


def halves(x):
    high = x.astype(BF16)
    return high, (x - high.astype(F32)).astype(BF16)


def kernel(
    n, m, heads,
    ld_hbm, gain_hbm, k_hbm, v_hbm, q_hbm, gate_hbm, grad_hbm,
    dq_hbm, dk_hbm, dv_hbm, dgate_hbm, dgain_hbm,
    ld, gain, k, v, q, gate, grad,
    dq, dk, dv, dgate, dgain,
    ld_rows, tri, cum_col, cum_row, grow, shrink,
    table, probs, dscores, attention, dnorm, closed, dattn, q_high, q_low, dk_part, dv_part,
    decay_out, decay_in, up_out, up_in, down_out, down_in,
    norm_out, norm_in, coefs, columns,
    back_up_out, back_up_in, back_down_out, back_down_in, gain_out, gain_in,
    in_sem, out_sem, send_sem, recv_sem,
):
    me, mt = lax.axis_index("ctx"), lax.axis_index("tp")
    per_head = n // heads
    channels = heads * HEAD * m
    width = heads * HEAD
    grad_rows = BLOCK // m

    loads = [
        pltpu.make_async_copy(src, dst, in_sem.at[i])
        for i, (src, dst) in enumerate(
            ((ld_hbm, ld), (k_hbm, k), (v_hbm, v), (q_hbm, q), (gate_hbm, gate), (gain_hbm, gain))
        )
    ]
    for load in loads:
        load.start()
    own_grad = pltpu.make_async_copy(
        grad_hbm.at[:, pl.ds(pl.multiple_of(mt * width, width), width)],
        grad.at[pl.ds(pl.multiple_of(mt * grad_rows, grad_rows), grad_rows), :],
        in_sem.at[6],
    )
    own_grad.start()

    def to_ctx(i):
        return lax.rem(me + i, n)

    def to_tp(i):
        return lax.rem(mt + i, m)

    barrier = pltpu.get_barrier_semaphore()

    @pl.loop(1, n)
    def _(i):
        pl.semaphore_signal(barrier, inc=1, device_id={"ctx": to_ctx(i), "tp": mt}, device_id_type=MESH)

    @pl.loop(1, m)
    def _(i):
        pl.semaphore_signal(barrier, inc=1, device_id={"ctx": me, "tp": to_tp(i)}, device_id_type=MESH)

    def send(src, dst, which, peer):
        pltpu.make_async_remote_copy(
            src_ref=src,
            dst_ref=dst,
            send_sem=send_sem.at[which],
            recv_sem=recv_sem.at[which],
            device_id=peer,
            device_id_type=MESH,
        ).start()

    def scatter(out, into, which):
        into[me] = out[me]

        @pl.loop(1, n)
        def _(i):
            peer = to_ctx(i)
            send(out.at[peer], into.at[me], which, {"ctx": peer, "tp": mt})

    def arrived(into, which, count):
        some = into.at[pl.ds(0, count)]
        pltpu.make_async_copy(some, some, recv_sem.at[which]).wait()

    def sent(out, which, count):
        some = out.at[pl.ds(0, count)]
        pltpu.make_async_copy(some, some, send_sem.at[which]).wait()

    t = lax.broadcasted_iota(jnp.int32, (BLOCK, BLOCK), 0)
    u = lax.broadcasted_iota(jnp.int32, (BLOCK, BLOCK), 1)
    tri[...] = jnp.where(t >= u, 1.0, 0.0).astype(BF16)
    ld_rows[...] = jnp.zeros_like(ld_rows)
    coefs[...] = jnp.zeros_like(coefs)
    loads[0].wait()
    ld_rows[0:heads, :] = ld[...]
    whole = ld_rows[...]
    part0 = whole.astype(BF16)
    rest = whole - part0.astype(F32)
    part1 = rest.astype(BF16)
    part2 = (rest - part1.astype(F32)).astype(BF16)
    col = dot(tri[...], part0, 1, 1) + dot(tri[...], part1, 1, 1) + dot(tri[...], part2, 1, 1)
    cum_col[...] = col
    last = col[BLOCK - 1 : BLOCK, :]
    grow[...] = jnp.exp(col)
    shrink[...] = jnp.exp(last - col)
    for h in range(heads):
        decay_out[h] = jnp.broadcast_to(jnp.exp(last[:, h : h + 1]), (1, HEAD))

    pl.semaphore_wait(barrier, n - 1 + m - 1)

    decay_in[me] = decay_out[me // per_head]

    @pl.loop(1, n)
    def _(i):
        peer = to_ctx(i)
        send(decay_out.at[peer // per_head], decay_in.at[me], DECAY, {"ctx": peer, "tp": mt})

    @pl.loop(1, m)
    def _(i):
        peer = to_tp(i)
        send(
            grad_hbm.at[:, pl.ds(pl.multiple_of(peer * width, width), width)],
            grad.at[pl.ds(pl.multiple_of(mt * grad_rows, grad_rows), grad_rows), :],
            GRAD,
            {"ctx": me, "tp": peer},
        )

    def cols(h):
        return slice(h * HEAD, (h + 1) * HEAD)

    def rows(r):
        return slice(r * CHUNK, (r + 1) * CHUNK)

    def state(ref, h):
        return ref[h * per_head : (h + 1) * per_head].reshape(HEAD, HEAD)

    loads[1].wait()
    loads[2].wait()
    for h in range(heads):
        high, low = halves(k[:, cols(h)].astype(F32) * shrink[:, h : h + 1])
        addend = dot(high, v[:, cols(h)], 0, 0) + dot(low, v[:, cols(h)], 0, 0)
        up_out[h * per_head : (h + 1) * per_head] = addend.astype(BF16).reshape(per_head, HEAD // per_head, HEAD)
    scatter(up_out, up_in, STATE_UP)

    cum_row[...] = dot(part0, tri[...], 1, 1) + dot(part1, tri[...], 1, 1) + dot(part2, tri[...], 1, 1)
    loads[3].wait()

    def inside(h):
        for r in range(CHUNKS):
            w = (r + 1) * CHUNK
            scores = dot(q[rows(r), cols(h)], k[0:w, cols(h)], 1, 1)
            spread = cum_col[rows(r), h : h + 1] - cum_row[h : h + 1, 0:w]
            at = lax.broadcasted_iota(jnp.int32, (CHUNK, w), 0) + r * CHUNK
            weight = jnp.where(
                at >= lax.broadcasted_iota(jnp.int32, (CHUNK, w), 1),
                jnp.exp(jnp.minimum(spread, 0.0)),
                0.0,
            )
            table[h, rows(r), 0:w] = weight
            p = (scores * weight).astype(BF16)
            probs[h, rows(r), 0:w] = p
            attention[rows(r), cols(h)] = dot(p, v[0:w, cols(h)], 1, 0)
        high, low = halves(q[:, cols(h)].astype(F32) * grow[:, h : h + 1])
        q_high[:, cols(h)] = high
        q_low[:, cols(h)] = low

    for h in range(heads // 2):
        inside(h)

    arrived(decay_in, DECAY, n - 1)
    arrived(up_in, STATE_UP, n - 1)
    carried = jnp.zeros(up_in.shape[1:], F32)
    for j in range(n):
        down_out[j] = carried.astype(BF16)
        carried = carried * decay_in[j] + up_in[j].astype(F32)
    scatter(down_out, down_in, STATE_DOWN)

    for h in range(heads // 2, heads):
        inside(h)
    loads[4].wait()
    loads[5].wait()
    own_grad.wait()
    arriving = grad.at[pl.ds(0, (m - 1) * grad_rows), :]
    pltpu.make_async_copy(arriving, arriving, recv_sem.at[GRAD]).wait()
    for r in range(CHUNKS):
        for h in range(heads):
            opened = jax.nn.sigmoid(gate[rows(r), cols(h)].astype(F32))
            dnorm[rows(r), cols(h)] = grad[rows(r), cols(h)].astype(F32) * opened
            closed[rows(r), cols(h)] = 1.0 - opened

    arrived(down_in, STATE_DOWN, n - 1)
    ones = jnp.ones((16, HEAD), BF16)
    for r in range(CHUNKS):
        squares = jnp.zeros((CHUNK, HEAD), F32)
        inner = jnp.zeros((CHUNK, HEAD), F32)
        for h in range(heads):
            a = attention[rows(r), cols(h)] + grow[rows(r), h : h + 1] * dot(
                q[rows(r), cols(h)], state(down_in, h), 1, 0
            )
            attention[rows(r), cols(h)] = a
            squares = squares + a * a
            inner = inner + a * (dnorm[rows(r), cols(h)] * gain[h : h + 1, :])
        for place, total in ((r, squares), (CHUNKS + r, inner)):
            high, low = halves(total)
            line = dot(ones, high, 1, 1) + dot(ones, low, 1, 1)
            norm_out[place : place + 1, :] = line[0:1, :]

    norm_in[mt] = norm_out[...]

    @pl.loop(1, m)
    def _(i):
        send(norm_out, norm_in.at[mt], NORM, {"ctx": me, "tp": to_tp(i)})

    arrived(norm_in, NORM, m - 1)
    total = norm_in[0]
    for j in range(1, m):
        total = total + norm_in[j]
    rscale = lax.rsqrt(total[0:CHUNKS] / channels + EPSILON)
    coefs[0:CHUNKS, :] = rscale
    coefs[CHUNKS : 2 * CHUNKS, :] = total[CHUNKS : 2 * CHUNKS] * (rscale * rscale * rscale) / channels
    columns[...] = jnp.transpose(coefs[...])

    for r in range(CHUNKS):
        scale, pull = columns[:, r : r + 1], columns[:, CHUNKS + r : CHUNKS + r + 1]
        for h in range(heads):
            d = dnorm[rows(r), cols(h)] * gain[h : h + 1, :] * scale - attention[rows(r), cols(h)] * pull
            dattn[rows(r), cols(h)] = d.astype(BF16)
    for h in range(heads):
        addend = dot(q_high[:, cols(h)], dattn[:, cols(h)], 0, 0) + dot(q_low[:, cols(h)], dattn[:, cols(h)], 0, 0)
        back_up_out[h * per_head : (h + 1) * per_head] = addend.astype(BF16).reshape(per_head, HEAD // per_head, HEAD)
    scatter(back_up_out, back_up_in, BACK_UP)

    for h in range(heads):
        part = jnp.zeros((1, HEAD), F32)
        for r in range(CHUNKS):
            x = dnorm[rows(r), cols(h)] * attention[rows(r), cols(h)] * columns[:, r : r + 1]
            dgate[rows(r), cols(h)] = (x * gain[h : h + 1, :] * closed[rows(r), cols(h)]).astype(BF16)
            part = part + jnp.sum(x, axis=0, keepdims=True)
        gain_out[h : h + 1, :] = part
    stores = [pltpu.make_async_copy(dgate, dgate_hbm, out_sem.at[0])]
    stores[0].start()
    gain_in[me] = gain_out[...]

    @pl.loop(1, n)
    def _(i):
        send(gain_out, gain_in.at[me], GAIN, {"ctx": to_ctx(i), "tp": mt})

    def backward(h):
        for r in range(CHUNKS):
            w = (r + 1) * CHUNK
            d = dattn[rows(r), cols(h)]
            ds = (dot(d, v[0:w, cols(h)], 1, 1) * table[h, rows(r), 0:w]).astype(BF16)
            dscores[h, rows(r), 0:w] = ds
            inter = grow[rows(r), h : h + 1] * dot(d, state(down_in, h), 1, 1)
            dq[rows(r), cols(h)] = (dot(ds, k[0:w, cols(h)], 1, 0) + inter).astype(BF16)
        for c in range(CHUNKS):
            later = slice(c * CHUNK, BLOCK)
            dk_part[rows(c), cols(h)] = dot(dscores[h, later, rows(c)], q[later, cols(h)], 0, 0)
            dv_part[rows(c), cols(h)] = dot(probs[h, later, rows(c)], dattn[later, cols(h)], 0, 0)

    for h in range(heads // 2):
        backward(h)

    arrived(back_up_in, BACK_UP, n - 1)
    carried = jnp.zeros(back_up_in.shape[1:], F32)
    for j in reversed(range(n)):
        back_down_out[j] = carried.astype(BF16)
        carried = carried * decay_in[j] + back_up_in[j].astype(F32)
    scatter(back_down_out, back_down_in, BACK_DOWN)

    for h in range(heads // 2, heads):
        backward(h)
    stores.append(pltpu.make_async_copy(dq, dq_hbm, out_sem.at[1]))
    stores[-1].start()

    arrived(gain_in, GAIN, n - 1)
    total = gain_in[0]
    for j in range(1, n):
        total = total + gain_in[j]
    dgain[...] = total
    stores.append(pltpu.make_async_copy(dgain, dgain_hbm, out_sem.at[2]))
    stores[-1].start()

    arrived(back_down_in, BACK_DOWN, n - 1)
    for h in range(heads):
        back = state(back_down_in, h)
        fade = shrink[:, h : h + 1]
        dk[:, cols(h)] = (dk_part[:, cols(h)] + fade * dot(v[:, cols(h)], back, 1, 1)).astype(BF16)
        dv[:, cols(h)] = (dv_part[:, cols(h)] + fade * dot(k[:, cols(h)], back, 1, 0)).astype(BF16)
    for i, (src, dst) in enumerate(((dk, dk_hbm), (dv, dv_hbm))):
        stores.append(pltpu.make_async_copy(src, dst, out_sem.at[3 + i]))
        stores[-1].start()

    sent(decay_in, DECAY, n - 1)
    pltpu.make_async_copy(arriving, arriving, send_sem.at[GRAD]).wait()
    sent(up_out, STATE_UP, n - 1)
    sent(down_out, STATE_DOWN, n - 1)
    sent(norm_in, NORM, m - 1)
    sent(back_up_out, BACK_UP, n - 1)
    sent(back_down_out, BACK_DOWN, n - 1)
    sent(gain_in, GAIN, n - 1)
    for store in stores:
        store.wait()


def local(n, m, queries, keys, values, log_decay, gate, gain, grad_out):
    heads = queries.shape[1] // HEAD
    width = heads * HEAD
    assert queries.shape[0] == BLOCK and n % heads == 0
    piece = (heads * HEAD // n, HEAD)
    square = (BLOCK, width)
    pairs = (heads, BLOCK, BLOCK)
    vmem = pltpu.VMEM
    outs = pl.pallas_call(
        functools.partial(kernel, n, m, heads),
        out_shape=[jax.ShapeDtypeStruct(square, BF16)] * 4 + [jax.ShapeDtypeStruct((heads, HEAD), F32)],
        in_specs=[pl.BlockSpec(memory_space=pl.ANY)] * 7,
        out_specs=[pl.BlockSpec(memory_space=pl.ANY)] * 5,
        scratch_shapes=[
            vmem((heads, BLOCK), F32), vmem((heads, HEAD), F32),
            *[vmem(square, BF16)] * 5,
            *[vmem(square, BF16)] * 4, vmem((heads, HEAD), F32),
            vmem((16, BLOCK), F32), vmem((BLOCK, BLOCK), BF16),
            vmem((BLOCK, 16), F32), vmem((16, BLOCK), F32), vmem((BLOCK, 16), F32), vmem((BLOCK, 16), F32),
            vmem(pairs, F32), vmem(pairs, BF16), vmem(pairs, BF16),
            *[vmem(square, F32)] * 3, *[vmem(square, BF16)] * 3, *[vmem(square, F32)] * 2,
            vmem((heads, 1, HEAD), F32), vmem((n, 1, HEAD), F32),
            *[vmem((n, *piece), BF16)] * 4,
            vmem((2 * CHUNKS, CHUNK), F32), vmem((m, 2 * CHUNKS, CHUNK), F32),
            vmem((CHUNK, CHUNK), F32), vmem((CHUNK, CHUNK), F32),
            *[vmem((n, *piece), BF16)] * 4,
            vmem((heads, HEAD), F32), vmem((n, heads, HEAD), F32),
            pltpu.SemaphoreType.DMA((7,)), pltpu.SemaphoreType.DMA((5,)),
            pltpu.SemaphoreType.DMA((8,)), pltpu.SemaphoreType.DMA((8,)),
        ],
        compiler_params=pltpu.CompilerParams(
            collective_id=0, has_side_effects=True, vmem_limit_bytes=48 << 20
        ),
    )(log_decay, gain.reshape(heads, HEAD), keys, values, queries, gate, grad_out)
    dq, dk, dv, dgate, dgain = outs
    return dq, dk, dv, dgate, dgain.reshape(width)


def solution(mesh):
    return jax.shard_map(
        functools.partial(local, mesh.shape["ctx"], mesh.shape["tp"]),
        mesh=mesh,
        in_specs=(
            P("ctx", "tp"),
            P("ctx", "tp"),
            P("ctx", "tp"),
            P("tp", "ctx"),
            P("ctx", "tp"),
            P("tp"),
            P(("ctx", "tp"), None),
        ),
        out_specs=(P("ctx", "tp"), P("ctx", "tp"), P("ctx", "tp"), P("ctx", "tp"), P("tp")),
        check_vma=False,
    )
```

time: 768 us -> 58.5 us (0.08)
  the two profiles are of different devices: /device:TPU:24 before, /device:TPU:1 now
where the time goes in v1:
time: 58.5 us; the launch traced here: 58.1 us
  Pallas kernels  47.1 us (81%)
  local copies, waits for them, and re-layouts  10.3 us (18%)
  between operations  0.66 us (1%)
    pallas_call x1, Pallas kernels, local(): pl.pallas_call(functools.partial(kernel, n, m, heads), out_shape=[jax.Sha...  47.1 us
    unnamed x19, local copies, waits for them, and re-layouts  10.3 us

profile of v1, /device:TPU:1, one launch (start us, length us, event | category | flops | bytes accessed | tf_op | source)
XLA Modules:
  0.0 58.1 jit_solution(7937423057936976569)
XLA Ops:
  0.6 0.0 copy-start
  0.6 1.0 %copy-done = bf16[512,512]{1,0:T(8,128)(2,1)S(1)} copy-done((bf16[512,512]{1,0:T(8,128)(2,1)S(1)}, bf16[512,512]{1,0:T(8,128)(2,1)}, u32[]{:S(2)}) %copy-start) | copy-done | bytes 524312
  1.7 0.0 copy-start.1
  1.7 1.0 %copy-done.1 = bf16[512,512]{1,0:T(8,128)(2,1)S(1)} copy-done((bf16[512,512]{1,0:T(8,128)(2,1)S(1)}, bf16[512,512]{1,0:T(8,128)(2,1)}, u32[]{:S(2)}) %copy-start.1) | copy-done | bytes 524312
  2.7 0.0 copy-start.2
  2.7 1.0 %copy-done.2 = bf16[512,512]{1,0:T(8,128)(2,1)S(1)} copy-done((bf16[512,512]{1,0:T(8,128)(2,1)S(1)}, bf16[512,512]{1,0:T(8,128)(2,1)}, u32[]{:S(2)}) %copy-start.2) | copy-done | bytes 524312
  3.8 0.0 copy-start.3
  3.8 1.0 %copy-done.3 = bf16[512,512]{1,0:T(8,128)(2,1)S(1)} copy-done((bf16[512,512]{1,0:T(8,128)(2,1)S(1)}, bf16[512,512]{1,0:T(8,128)(2,1)}, u32[]{:S(2)}) %copy-start.3) | copy-done | bytes 524312
  4.8 0.0 copy-start.4
  4.8 1.0 %copy-done.4 = bf16[64,4096]{1,0:T(8,128)(2,1)S(1)} copy-done((bf16[64,4096]{1,0:T(8,128)(2,1)S(1)}, bf16[64,4096]{1,0:T(8,128)(2,1)}, u32[]{:S(2)}) %copy-start.4) | copy-done | bytes 524312
  5.8 0.0 copy-start.5
  5.8 0.7 %copy-done.5 = f32[4,512]{1,0:T(4,128)S(1)} copy-done((f32[4,512]{1,0:T(4,128)S(1)}, f32[4,512]{1,0:T(4,128)}, u32[]{:S(2)}) %copy-start.5) | copy-done | bytes 8216
  6.5 0.0 copy-start.6
  6.5 0.7 %copy-done.6 = f32[512]{0:T(512)S(1)} copy-done((f32[512]{0:T(512)S(1)}, f32[512]{0:T(512)}, u32[]{:S(2)}) %copy-start.6) | copy-done | bytes 2072
  7.2 47.1 %shard_map.110 = (bf16[512,512]{1,0:T(8,128)(2,1)S(1)}, bf16[512,512]{1,0:T(8,128)(2,1)S(1)}, bf16[512,512]{1,0:T(8,128)(2,1)S(1)}, bf16[512,512]{1,0:T(8,128)(2,1)S(1)}, f32[4,128]{1,0:T(4,128)S(1)}) custom-call(f32[4,512]{1,0:T(4,128)S(1)} %copy-done.5, f32[4,128]{1,0:T(4,128)S(1)} %bitcast.3, bf16[512,512]{1,0:T(8,128)(2,1)S(1)} %copy-done, ...), custom_call_target="tpu_custom_call" | custom-call | tf_op jit(solution)/shard_map/pallas_call | solution.py:333
  54.4 0.8 %copy.17 = bf16[512,512]{1,0:T(8,128)(2,1)} copy(bf16[512,512]{1,0:T(8,128)(2,1)S(1)} %get-tuple-element.20) | data formatting | bytes 1048576
  55.2 0.8 %copy.18 = bf16[512,512]{1,0:T(8,128)(2,1)} copy(bf16[512,512]{1,0:T(8,128)(2,1)S(1)} %get-tuple-element.21) | data formatting | bytes 1048576
  56.0 0.8 %copy.19 = bf16[512,512]{1,0:T(8,128)(2,1)} copy(bf16[512,512]{1,0:T(8,128)(2,1)S(1)} %get-tuple-element.22) | data formatting | bytes 1048576
  56.8 0.8 %copy.20 = bf16[512,512]{1,0:T(8,128)(2,1)} copy(bf16[512,512]{1,0:T(8,128)(2,1)S(1)} %get-tuple-element.23) | data formatting | bytes 1048576
  57.6 0.6 copy.21
Async XLA Ops:
  0.6 1.0 %copy-start = (bf16[512,512]{1,0:T(8,128)(2,1)S(1)}, bf16[512,512]{1,0:T(8,128)(2,1)}, u32[]{:S(2)}) copy-start(bf16[512,512]{1,0:T(8,128)(2,1)} %k_hbm.1) | copy-start | bytes 1572868
  1.7 1.0 %copy-start.1 = (bf16[512,512]{1,0:T(8,128)(2,1)S(1)}, bf16[512,512]{1,0:T(8,128)(2,1)}, u32[]{:S(2)}) copy-start(bf16[512,512]{1,0:T(8,128)(2,1)} %v_hbm.1) | copy-start | bytes 1572868
  2.7 1.0 %copy-start.2 = (bf16[512,512]{1,0:T(8,128)(2,1)S(1)}, bf16[512,512]{1,0:T(8,128)(2,1)}, u32[]{:S(2)}) copy-start(bf16[512,512]{1,0:T(8,128)(2,1)} %q_hbm.1) | copy-start | bytes 1572868
  3.8 1.0 %copy-start.3 = (bf16[512,512]{1,0:T(8,128)(2,1)S(1)}, bf16[512,512]{1,0:T(8,128)(2,1)}, u32[]{:S(2)}) copy-start(bf16[512,512]{1,0:T(8,128)(2,1)} %gate_hbm.1) | copy-start | bytes 1572868
  4.8 1.0 %copy-start.4 = (bf16[64,4096]{1,0:T(8,128)(2,1)S(1)}, bf16[64,4096]{1,0:T(8,128)(2,1)}, u32[]{:S(2)}) copy-start(bf16[64,4096]{1,0:T(8,128)(2,1)} %grad_hbm.1) | copy-start | bytes 1572868
  5.8 0.7 %copy-start.5 = (f32[4,512]{1,0:T(4,128)S(1)}, f32[4,512]{1,0:T(4,128)}, u32[]{:S(2)}) copy-start(f32[4,512]{1,0:T(4,128)} %ld_hbm.1) | copy-start | bytes 24580
  6.5 0.7 %copy-start.6 = (f32[512]{0:T(512)S(1)}, f32[512]{0:T(512)}, u32[]{:S(2)}) copy-start(f32[512]{0:T(512)} %param.12) | copy-start | bytes 6148

commit v2 on v1

v2 whole, which is shorter than its diff:
```python
import functools

import jax
import jax.numpy as jnp
from jax import lax
from jax.experimental import pallas as pl
from jax.experimental.pallas import tpu as pltpu
from jax.sharding import PartitionSpec as P

HEAD = 128
BLOCK = 512
CHUNK = 128
CHUNKS = BLOCK // CHUNK
EPSILON = 1e-06
MESH = pl.DeviceIdType.MESH
F32, BF16 = jnp.float32, jnp.bfloat16

DECAY_PAIR, DECAY, GRAD, NORM, GAIN_PAIR, GAIN, FORWARD, BACKWARD = 0, 1, 2, 3, 4, 5, 6, 11
URGENT, REST, UP, DOWN, WHOLE = range(5)
SEMAPHORES = 16


def dot(a, b, over_a, over_b):
    return lax.dot_general(
        a, b, (((over_a,), (over_b,)), ((), ())), preferred_element_type=F32
    )


def halves(x):
    high = x.astype(BF16)
    return high, (x - high.astype(F32)).astype(BF16)


def far_first(count):
    return sorted(range(count), key=lambda i: -min(i, count - i))


def kernel(
    n, m, heads,
    ld_hbm, gain_hbm, k_hbm, v_hbm, q_hbm, gate_hbm, grad_hbm,
    dq, dk, dv, dgate, dgain,
    ld, gain, k, v, q, gate, grad,
    ld_rows, tri, cum_col, cum_row, grow, shrink,
    table, probs, dscores, attention, dnorm, closed, dattn, q_high, q_low, dk_part, dv_part,
    decay_own, decay_pair, decay_out, decay_in,
    norm_out, norm_in, coefs, columns, gain_own, gain_pair, gain_in,
    fore_own, fore_out, fore_pair, fore_up_out, fore_up_in, fore_down, fore_whole, fore_state,
    back_own, back_out, back_pair, back_up_out, back_up_in, back_down, back_whole,
    in_sem, send_sem, recv_sem,
):
    me, mt = lax.axis_index("ctx"), lax.axis_index("tp")
    core, chip = lax.rem(me, 2), me // 2
    chips, deep = n // 2, n // 4
    per_head = n // heads
    channels = heads * HEAD * m
    width = heads * HEAD
    grad_rows = BLOCK // m
    half = pl.ds(core * chips, chips)
    other_half = pl.ds((1 - core) * chips, chips)

    loads = [
        pltpu.make_async_copy(src, dst, in_sem.at[i])
        for i, (src, dst) in enumerate(
            ((ld_hbm, ld), (k_hbm, k), (v_hbm, v), (q_hbm, q), (gate_hbm, gate), (gain_hbm, gain))
        )
    ]
    for load in loads:
        load.start()

    peers = [
        lax.rem(chip // deep + y, 2) * deep + lax.rem(chip + z, deep)
        for z in far_first(deep)
        for y in (1, 0)
        if (y, z) != (0, 0)
    ]
    tp_peers = [
        lax.rem(mt // 2 + x, m // 2) * 2 + lax.rem(mt + y, 2)
        for y in (1, 0)
        for x in far_first(m // 2)
        if (y, x) != (0, 0)
    ]

    def on_chip(p):
        return {"ctx": 2 * p + core, "tp": mt}

    def on_tp(p):
        return {"ctx": me, "tp": p}

    sibling = {"ctx": 2 * chip + 1 - core, "tp": mt}

    barrier = pltpu.get_barrier_semaphore()
    greeted = [on_chip(p) for p in peers] + [on_tp(p) for p in tp_peers] + [sibling]
    for device in greeted:
        pl.semaphore_signal(barrier, inc=1, device_id=device, device_id_type=MESH)

    def send(src, dst, which, device):
        pltpu.make_async_remote_copy(
            src_ref=src,
            dst_ref=dst,
            send_sem=send_sem.at[which],
            recv_sem=recv_sem.at[which],
            device_id=device,
            device_id_type=MESH,
        ).start()

    def arrived(some, which):
        pltpu.make_async_copy(some, some, recv_sem.at[which]).wait()

    def sent(some, which):
        pltpu.make_async_copy(some, some, send_sem.at[which]).wait()

    def cols(h):
        return slice(h * HEAD, (h + 1) * HEAD)

    def rows(r):
        return slice(r * CHUNK, (r + 1) * CHUNK)

    def pieces(h):
        return slice(h * per_head, (h + 1) * per_head)

    def state(ref, h):
        return ref[pieces(h)].reshape(HEAD, HEAD)

    t = lax.broadcasted_iota(jnp.int32, (BLOCK, BLOCK), 0)
    u = lax.broadcasted_iota(jnp.int32, (BLOCK, BLOCK), 1)
    tri[...] = jnp.where(t >= u, 1.0, 0.0).astype(BF16)
    ld_rows[...] = jnp.zeros_like(ld_rows)
    coefs[...] = jnp.zeros_like(coefs)
    loads[0].wait()
    ld_rows[0:heads, :] = ld[...]
    whole = ld_rows[...]
    part0 = whole.astype(BF16)
    rest = whole - part0.astype(F32)
    part1 = rest.astype(BF16)
    part2 = (rest - part1.astype(F32)).astype(BF16)
    col = dot(tri[...], part0, 1, 1) + dot(tri[...], part1, 1, 1) + dot(tri[...], part2, 1, 1)
    cum_col[...] = col
    last = col[BLOCK - 1 : BLOCK, :]
    grow[...] = jnp.exp(col)
    shrink[...] = jnp.exp(last - col)
    for h in range(heads):
        decay_own[h] = jnp.broadcast_to(jnp.exp(last[:, h : h + 1]), (1, HEAD))

    pl.semaphore_wait(barrier, len(greeted))
    send(decay_own, decay_pair, DECAY_PAIR, sibling)

    def share(h, addend, own, out):
        addend = addend.reshape(per_head, HEAD // per_head, HEAD)
        own[pieces(h)] = addend
        out[pieces(h)] = addend.astype(BF16)

    def swap(out, pair, first):
        send(out.at[other_half], pair.at[other_half], first + URGENT, sibling)
        send(out.at[half], pair.at[half], first + REST, sibling)

    def join(own, pair, up_out, up_in, leads, first):
        arrived(pair.at[half], first + URGENT)
        for g in range(heads // 2):
            h = core * (heads // 2) + g
            here = pl.ds(core * chips + g * per_head, per_head)
            by_own = leads * decay_pair[h] + (1.0 - leads)
            by_pair = leads + (1.0 - leads) * decay_own[h]
            up_out[pieces(g)] = (own[here] * by_own + pair[here].astype(F32) * by_pair).astype(BF16)
        for p in peers:
            send(up_out.at[p], up_in.at[chip], first + UP, on_chip(p))
        up_in[chip] = up_out[chip]

    def scan(up_in, down, whole, order, first):
        arrived(up_in.at[pl.ds(0, chips - 1)], first + UP)
        carried = jnp.zeros(up_in.shape[1:], F32)
        for j in order:
            down[j] = carried.astype(BF16)
            carried = carried * decay_in[j] + up_in[j].astype(F32)
        for p in peers:
            send(down.at[p], whole.at[core * chips + chip], first + DOWN, on_chip(p))
        whole[core * chips + chip] = down[chip]

    def settle(whole, pair, first):
        arrived(whole.at[pl.ds(0, chips - 1)], first + DOWN)
        send(whole.at[half], whole.at[half], first + WHOLE, sibling)
        arrived(pair.at[other_half], first + REST)
        arrived(whole.at[other_half], first + WHOLE)

    def entering(whole, pair, leads, h):
        by_chip = leads + (1.0 - leads) * decay_pair[h]
        held = whole[pieces(h)].astype(F32) * by_chip + pair[pieces(h)].astype(F32) * (1.0 - leads)
        return held.astype(BF16)

    fore_leads = (1 - core).astype(F32)
    back_leads = core.astype(F32)

    loads[1].wait()
    loads[2].wait()
    for h in range(heads):
        high, low = halves(k[:, cols(h)].astype(F32) * shrink[:, h : h + 1])
        share(h, dot(high, v[:, cols(h)], 0, 0) + dot(low, v[:, cols(h)], 0, 0), fore_own, fore_out)
    swap(fore_out, fore_pair, FORWARD)

    arrived(decay_pair, DECAY_PAIR)
    decay_out[...] = decay_own[...] * decay_pair[...]
    for p in peers:
        send(decay_out.at[(core * chips + p) // per_head], decay_in.at[chip], DECAY, on_chip(p))
    decay_in[chip] = decay_out[(core * chips + chip) // per_head]
    join(fore_own, fore_pair, fore_up_out, fore_up_in, fore_leads, FORWARD)

    def grad_part(p):
        return grad_hbm.at[:, pl.ds(pl.multiple_of(p * width, width), width)]

    grad_place = grad.at[pl.ds(pl.multiple_of(mt * grad_rows, grad_rows), grad_rows), :]
    own_grad = pltpu.make_async_copy(grad_part(mt), grad_place, in_sem.at[6])
    own_grad.start()
    for p in tp_peers:
        send(grad_part(p), grad_place, GRAD, on_tp(p))

    cum_row[...] = dot(part0, tri[...], 1, 1) + dot(part1, tri[...], 1, 1) + dot(part2, tri[...], 1, 1)
    loads[3].wait()

    def inside(h):
        for r in range(CHUNKS):
            w = (r + 1) * CHUNK
            scores = dot(q[rows(r), cols(h)], k[0:w, cols(h)], 1, 1)
            spread = cum_col[rows(r), h : h + 1] - cum_row[h : h + 1, 0:w]
            at = lax.broadcasted_iota(jnp.int32, (CHUNK, w), 0) + r * CHUNK
            weight = jnp.where(
                at >= lax.broadcasted_iota(jnp.int32, (CHUNK, w), 1),
                jnp.exp(jnp.minimum(spread, 0.0)),
                0.0,
            )
            table[h, rows(r), 0:w] = weight
            p = (scores * weight).astype(BF16)
            probs[h, rows(r), 0:w] = p
            attention[rows(r), cols(h)] = dot(p, v[0:w, cols(h)], 1, 0)
        high, low = halves(q[:, cols(h)].astype(F32) * grow[:, h : h + 1])
        q_high[cols(h), :] = jnp.transpose(high)
        q_low[cols(h), :] = jnp.transpose(low)

    for h in range(heads // 2):
        inside(h)

    arrived(decay_in.at[pl.ds(0, chips - 1)], DECAY)
    scan(fore_up_in, fore_down, fore_whole, range(chips), FORWARD)

    for h in range(heads // 2, heads):
        inside(h)
    loads[4].wait()
    loads[5].wait()
    own_grad.wait()
    arriving = grad.at[pl.ds(0, (m - 1) * grad_rows), :]
    arrived(arriving, GRAD)
    for r in range(CHUNKS):
        for h in range(heads):
            opened = jax.nn.sigmoid(gate[rows(r), cols(h)].astype(F32))
            dnorm[rows(r), cols(h)] = grad[rows(r), cols(h)].astype(F32) * opened
            closed[rows(r), cols(h)] = 1.0 - opened

    settle(fore_whole, fore_pair, FORWARD)
    for h in range(heads):
        fore_state[pieces(h)] = entering(fore_whole, fore_pair, fore_leads, h)
    ones = jnp.ones((16, HEAD), BF16)
    for r in range(CHUNKS):
        squares = jnp.zeros((CHUNK, HEAD), F32)
        inner = jnp.zeros((CHUNK, HEAD), F32)
        for h in range(heads):
            a = attention[rows(r), cols(h)] + grow[rows(r), h : h + 1] * dot(
                q[rows(r), cols(h)], state(fore_state, h), 1, 0
            )
            attention[rows(r), cols(h)] = a
            squares = squares + a * a
            inner = inner + a * (dnorm[rows(r), cols(h)] * gain[h : h + 1, :])
        for place, total in ((r, squares), (CHUNKS + r, inner)):
            high, low = halves(total)
            line = dot(ones, high, 1, 1) + dot(ones, low, 1, 1)
            norm_out[place : place + 1, :] = line[0:1, :]
    for p in tp_peers:
        send(norm_out, norm_in.at[mt], NORM, on_tp(p))
    norm_in[mt] = norm_out[...]
    arrived(norm_in.at[pl.ds(0, m - 1)], NORM)
    total = norm_in[0]
    for j in range(1, m):
        total = total + norm_in[j]
    rscale = lax.rsqrt(total[0:CHUNKS] / channels + EPSILON)
    coefs[0:CHUNKS, :] = rscale
    coefs[CHUNKS : 2 * CHUNKS, :] = total[CHUNKS : 2 * CHUNKS] * (rscale * rscale * rscale) / channels
    columns[...] = jnp.transpose(coefs[...])

    for r in range(CHUNKS):
        scale, pull = columns[:, r : r + 1], columns[:, CHUNKS + r : CHUNKS + r + 1]
        for h in range(heads):
            d = dnorm[rows(r), cols(h)] * gain[h : h + 1, :] * scale - attention[rows(r), cols(h)] * pull
            dattn[rows(r), cols(h)] = d.astype(BF16)
    for h in range(heads):
        share(h, dot(q_high[cols(h), :], dattn[:, cols(h)], 1, 0) + dot(q_low[cols(h), :], dattn[:, cols(h)], 1, 0), back_own, back_out)
    swap(back_out, back_pair, BACKWARD)

    for h in range(heads):
        part = jnp.zeros((1, HEAD), F32)
        for r in range(CHUNKS):
            x = dnorm[rows(r), cols(h)] * attention[rows(r), cols(h)] * columns[:, r : r + 1]
            dgate[rows(r), cols(h)] = (x * gain[h : h + 1, :] * closed[rows(r), cols(h)]).astype(BF16)
            part = part + jnp.sum(x, axis=0, keepdims=True)
        gain_own[h : h + 1, :] = part
    send(gain_own, gain_pair, GAIN_PAIR, sibling)
    join(back_own, back_pair, back_up_out, back_up_in, back_leads, BACKWARD)

    def backward(h):
        for r in range(CHUNKS):
            w = (r + 1) * CHUNK
            d = dattn[rows(r), cols(h)]
            ds = (dot(d, v[0:w, cols(h)], 1, 1) * table[h, rows(r), 0:w]).astype(BF16)
            dscores[h, rows(r), 0:w] = ds
            inter = grow[rows(r), h : h + 1] * dot(d, state(fore_state, h), 1, 1)
            dq[rows(r), cols(h)] = (dot(ds, k[0:w, cols(h)], 1, 0) + inter).astype(BF16)
        for c in range(CHUNKS):
            later = slice(c * CHUNK, BLOCK)
            dk_part[rows(c), cols(h)] = dot(dscores[h, later, rows(c)], q[later, cols(h)], 0, 0)
            dv_part[rows(c), cols(h)] = dot(probs[h, later, rows(c)], dattn[later, cols(h)], 0, 0)

    backward(0)
    arrived(gain_pair, GAIN_PAIR)
    gain_in[chip] = gain_own[...] + gain_pair[...]
    for p in peers:
        send(gain_in.at[chip], gain_in.at[chip], GAIN, on_chip(p))
    for h in range(1, heads // 2):
        backward(h)

    scan(back_up_in, back_down, back_whole, reversed(range(chips)), BACKWARD)

    for h in range(heads // 2, heads):
        backward(h)

    arrived(gain_in.at[pl.ds(0, chips - 1)], GAIN)
    total = gain_in[0]
    for j in range(1, chips):
        total = total + gain_in[j]
    dgain[...] = total

    settle(back_whole, back_pair, BACKWARD)
    for h in range(heads):
        back = entering(back_whole, back_pair, back_leads, h).reshape(HEAD, HEAD)
        fade = shrink[:, h : h + 1]
        dk[:, cols(h)] = (dk_part[:, cols(h)] + fade * dot(v[:, cols(h)], back, 1, 1)).astype(BF16)
        dv[:, cols(h)] = (dv_part[:, cols(h)] + fade * dot(k[:, cols(h)], back, 1, 0)).astype(BF16)

    sent(decay_own, DECAY_PAIR)
    sent(decay_in.at[pl.ds(0, chips - 1)], DECAY)
    sent(arriving, GRAD)
    sent(norm_in.at[pl.ds(0, m - 1)], NORM)
    sent(gain_own, GAIN_PAIR)
    sent(gain_in.at[pl.ds(0, chips - 1)], GAIN)
    for first, up_out in ((FORWARD, fore_up_out), (BACKWARD, back_up_out)):
        one_less = up_out.at[pl.ds(0, chips - 1)]
        for which, some in ((URGENT, up_out), (REST, up_out), (UP, one_less), (DOWN, one_less), (WHOLE, up_out)):
            sent(some, first + which)


def put(*refs):
    sem, half = refs[-1], len(refs) // 2
    copies = [pltpu.make_async_copy(refs[i], refs[half + i], sem.at[i]) for i in range(half)]
    for copy in copies:
        copy.start()
    for copy in copies:
        copy.wait()


def local(n, m, queries, keys, values, log_decay, gate, gain, grad_out):
    heads = queries.shape[1] // HEAD
    width = heads * HEAD
    assert queries.shape[0] == BLOCK and n % heads == 0
    piece = (heads * HEAD // n, HEAD)
    square = (BLOCK, width)
    pairs = (heads, BLOCK, BLOCK)
    vmem = pltpu.VMEM
    sweep = [
        vmem((n, *piece), F32), *[vmem((n, *piece), BF16)] * 2,
        *[vmem((n // 2, *piece), BF16)] * 3, vmem((n, *piece), BF16),
    ]
    outs = pl.pallas_call(
        functools.partial(kernel, n, m, heads),
        out_shape=[jax.ShapeDtypeStruct(square, BF16)] * 4 + [jax.ShapeDtypeStruct((heads, HEAD), F32)],
        in_specs=[pl.BlockSpec(memory_space=pltpu.HBM)] * 7,
        out_specs=[pl.BlockSpec(memory_space=pltpu.VMEM)] * 5,
        scratch_shapes=[
            vmem((heads, BLOCK), F32), vmem((heads, HEAD), F32),
            *[vmem(square, BF16)] * 5,
            vmem((16, BLOCK), F32), vmem((BLOCK, BLOCK), BF16),
            vmem((BLOCK, 16), F32), vmem((16, BLOCK), F32), vmem((BLOCK, 16), F32), vmem((BLOCK, 16), F32),
            vmem(pairs, F32), vmem(pairs, BF16), vmem(pairs, BF16),
            *[vmem(square, F32)] * 3, vmem(square, BF16), *[vmem((width, BLOCK), BF16)] * 2, *[vmem(square, F32)] * 2,
            *[vmem((heads, 1, HEAD), F32)] * 3, vmem((n // 2, 1, HEAD), F32),
            vmem((2 * CHUNKS, CHUNK), F32), vmem((m, 2 * CHUNKS, CHUNK), F32),
            vmem((CHUNK, CHUNK), F32), vmem((CHUNK, CHUNK), F32),
            *[vmem((heads, HEAD), F32)] * 2, vmem((n // 2, heads, HEAD), F32),
            *sweep, vmem((n, *piece), BF16),
            *sweep,
            pltpu.SemaphoreType.DMA((7,)),
            pltpu.SemaphoreType.DMA((SEMAPHORES,)), pltpu.SemaphoreType.DMA((SEMAPHORES,)),
        ],
        compiler_params=pltpu.CompilerParams(
            collective_id=0, has_side_effects=True, vmem_limit_bytes=48 << 20
        ),
    )(*[pltpu.with_memory_space_constraint(x, pltpu.HBM) for x in (log_decay, gain.reshape(heads, HEAD), keys, values, queries, gate, grad_out)])
    dq, dk, dv, dgate, dgain = pl.pallas_call(
        put,
        out_shape=[jax.ShapeDtypeStruct(x.shape, x.dtype) for x in outs],
        in_specs=[pl.BlockSpec(memory_space=pl.ANY)] * len(outs),
        out_specs=[pl.BlockSpec(memory_space=pltpu.HBM)] * len(outs),
        scratch_shapes=[pltpu.SemaphoreType.DMA((len(outs),))],
    )(*[pltpu.with_memory_space_constraint(x, pltpu.VMEM) for x in outs])
    return dq, dk, dv, dgate, dgain.reshape(width)


def solution(mesh):
    return jax.shard_map(
        functools.partial(local, mesh.shape["ctx"], mesh.shape["tp"]),
        mesh=mesh,
        in_specs=(
            P("ctx", "tp"),
            P("ctx", "tp"),
            P("ctx", "tp"),
            P("tp", "ctx"),
            P("ctx", "tp"),
            P("tp"),
            P(("ctx", "tp"), None),
        ),
        out_specs=(P("ctx", "tp"), P("ctx", "tp"), P("ctx", "tp"), P("ctx", "tp"), P("tp")),
        check_vma=False,
    )
```

time: 58.5 us -> 47.1 us (0.81)
  local copies, waits for them, and re-layouts: 10.3 us -> 0 us
  Pallas kernels: 47.1 us -> 46.4 us
    unnamed x19 -> x0, local copies, waits for them, and re-layouts: 10.3 us -> none
    pallas_call x1, Pallas kernels: 47.1 us -> 45 us  [local(): pl.pallas_call(functools.partial(kernel, n, m, heads), out_shape=[jax.Sha...]
    pallas_call x0 -> x1, Pallas kernels: none -> 1.36 us  [local(): pl.pallas_call(put, out_shape=[jax.ShapeDtypeStruct(x.shape, x.dtype) for...]
where the time goes in v2:
time: 47.1 us; the launch traced here: 47 us
  Pallas kernels  46.4 us (99%)
  between operations  0.64 us (1%)
    pallas_call x1, Pallas kernels, local(): pl.pallas_call(functools.partial(kernel, n, m, heads), out_shape=[jax.Sha...  45 us
    pallas_call x1, Pallas kernels, local(): pl.pallas_call(put, out_shape=[jax.ShapeDtypeStruct(x.shape, x.dtype) for...  1.36 us

profile of v2, /device:TPU:1, one launch (start us, length us, event | category | flops | bytes accessed | tf_op | source)
XLA Modules:
  0.0 47.0 jit_solution(7216741422621117554)
XLA Ops:
  0.6 45.0 %shard_map.110 = (bf16[512,512]{1,0:T(8,128)(2,1)S(1)}, bf16[512,512]{1,0:T(8,128)(2,1)S(1)}, bf16[512,512]{1,0:T(8,128)(2,1)S(1)}, bf16[512,512]{1,0:T(8,128)(2,1)S(1)}, f32[4,128]{1,0:T(4,128)S(1)}) custom-call(f32[4,512]{1,0:T(4,128)} %ld_hbm.1, f32[4,128]{1,0:T(4,128)} %bitcast.2, bf16[512,512]{1,0:T(8,128)(2,1)} %k_hbm.1, bf16[512,512]{1,0:T(8,128)(2,1)} %v_hbm.1, ...), custom_call_target="tpu_custom_call" | custom-call | tf_op jit(solution)/shard_map/pallas_call | solution.py:377
  45.6 1.4 %shard_map.111 = (bf16[512,512]{1,0:T(8,128)(2,1)}, bf16[512,512]{1,0:T(8,128)(2,1)}, bf16[512,512]{1,0:T(8,128)(2,1)}, bf16[512,512]{1,0:T(8,128)(2,1)}, f32[4,128]{1,0:T(4,128)}) custom-call(bf16[512,512]{1,0:T(8,128)(2,1)S(1)} %get-tuple-element.15.refs_0_, bf16[512,512]{1,0:T(8,128)(2,1)S(1)} %get-tuple-element.16.refs_1_, ...), custom_call_target="tpu_custom_call" | custom-call | tf_op jit(solution)/shard_map/pallas_call | solution.py:402

commit v3 on v2

--- a/solution.py
+++ b/solution.py
@@ -38,10 +38,10 @@
 def kernel(
     n, m, heads,
     ld_hbm, gain_hbm, k_hbm, v_hbm, q_hbm, gate_hbm, grad_hbm,
-    dq, dk, dv, dgate, dgain,
-    ld, gain, k, v, q, gate, grad,
-    ld_rows, tri, cum_col, cum_row, grow, shrink,
-    table, probs, dscores, attention, dnorm, closed, dattn, q_high, q_low, dk_part, dv_part,
+    dq, dgate, dgain, k, v, shrink, back_state, dk_part, dv_part,
+    ld, gain, q, gate, grad,
+    ld_rows, tri, cum_col, cum_row, grow,
+    table, probs, dscores, attention, dnorm, closed, dattn, q_high, q_low,
     decay_own, decay_pair, decay_out, decay_in,
     norm_out, norm_in, coefs, columns, gain_own, gain_pair, gain_in,
     fore_own, fore_out, fore_pair, fore_up_out, fore_up_in, fore_down, fore_whole, fore_state,
@@ -141,9 +141,6 @@
     for h in range(heads):
         decay_own[h] = jnp.broadcast_to(jnp.exp(last[:, h : h + 1]), (1, HEAD))
 
-    pl.semaphore_wait(barrier, len(greeted))
-    send(decay_own, decay_pair, DECAY_PAIR, sibling)
-
     def share(h, addend, own, out):
         addend = addend.reshape(per_head, HEAD // per_head, HEAD)
         own[pieces(h)] = addend
@@ -194,7 +191,18 @@
     for h in range(heads):
         high, low = halves(k[:, cols(h)].astype(F32) * shrink[:, h : h + 1])
         share(h, dot(high, v[:, cols(h)], 0, 0) + dot(low, v[:, cols(h)], 0, 0), fore_own, fore_out)
+    pl.semaphore_wait(barrier, len(greeted))
+    send(decay_own, decay_pair, DECAY_PAIR, sibling)
     swap(fore_out, fore_pair, FORWARD)
+
+    def grad_part(p):
+        return grad_hbm.at[:, pl.ds(pl.multiple_of(p * width, width), width)]
+
+    grad_place = grad.at[pl.ds(pl.multiple_of(mt * grad_rows, grad_rows), grad_rows), :]
+    own_grad = pltpu.make_async_copy(grad_part(mt), grad_place, in_sem.at[6])
+    own_grad.start()
+    for p in tp_peers:
+        send(grad_part(p), grad_place, GRAD, on_tp(p))
 
     arrived(decay_pair, DECAY_PAIR)
     decay_out[...] = decay_own[...] * decay_pair[...]
@@ -202,15 +210,6 @@
         send(decay_out.at[(core * chips + p) // per_head], decay_in.at[chip], DECAY, on_chip(p))
     decay_in[chip] = decay_out[(core * chips + chip) // per_head]
     join(fore_own, fore_pair, fore_up_out, fore_up_in, fore_leads, FORWARD)
-
-    def grad_part(p):
-        return grad_hbm.at[:, pl.ds(pl.multiple_of(p * width, width), width)]
-
-    grad_place = grad.at[pl.ds(pl.multiple_of(mt * grad_rows, grad_rows), grad_rows), :]
-    own_grad = pltpu.make_async_copy(grad_part(mt), grad_place, in_sem.at[6])
-    own_grad.start()
-    for p in tp_peers:
-        send(grad_part(p), grad_place, GRAD, on_tp(p))
 
     cum_row[...] = dot(part0, tri[...], 1, 1) + dot(part1, tri[...], 1, 1) + dot(part2, tri[...], 1, 1)
     loads[3].wait()
@@ -315,15 +314,14 @@
             dk_part[rows(c), cols(h)] = dot(dscores[h, later, rows(c)], q[later, cols(h)], 0, 0)
             dv_part[rows(c), cols(h)] = dot(probs[h, later, rows(c)], dattn[later, cols(h)], 0, 0)
 
-    backward(0)
+    for h in range(heads // 2):
+        backward(h)
     arrived(gain_pair, GAIN_PAIR)
     gain_in[chip] = gain_own[...] + gain_pair[...]
+
+    scan(back_up_in, back_down, back_whole, reversed(range(chips)), BACKWARD)
     for p in peers:
         send(gain_in.at[chip], gain_in.at[chip], GAIN, on_chip(p))
-    for h in range(1, heads // 2):
-        backward(h)
-
-    scan(back_up_in, back_down, back_whole, reversed(range(chips)), BACKWARD)
 
     for h in range(heads // 2, heads):
         backward(h)
@@ -336,10 +334,7 @@
 
     settle(back_whole, back_pair, BACKWARD)
     for h in range(heads):
-        back = entering(back_whole, back_pair, back_leads, h).reshape(HEAD, HEAD)
-        fade = shrink[:, h : h + 1]
-        dk[:, cols(h)] = (dk_part[:, cols(h)] + fade * dot(v[:, cols(h)], back, 1, 1)).astype(BF16)
-        dv[:, cols(h)] = (dv_part[:, cols(h)] + fade * dot(k[:, cols(h)], back, 1, 0)).astype(BF16)
+        back_state[pieces(h)] = entering(back_whole, back_pair, back_leads, h)
 
     sent(decay_own, DECAY_PAIR)
     sent(decay_in.at[pl.ds(0, chips - 1)], DECAY)
@@ -353,11 +348,29 @@
             sent(some, first + which)
 
 
-def put(*refs):
-    sem, half = refs[-1], len(refs) // 2
-    copies = [pltpu.make_async_copy(refs[i], refs[half + i], sem.at[i]) for i in range(half)]
+def finish(
+    dq, dgate, dgain, k, v, shrink, back_state, dk_part, dv_part,
+    dq_hbm, dgate_hbm, dgain_hbm, dk_hbm, dv_hbm,
+    dk, dv, sem,
+):
+    heads = dgain.shape[0]
+    per_head = back_state.shape[0] // heads
+    copies = [
+        pltpu.make_async_copy(src, dst, sem.at[i])
+        for i, (src, dst) in enumerate(((dq, dq_hbm), (dgate, dgate_hbm), (dgain, dgain_hbm)))
+    ]
     for copy in copies:
         copy.start()
+    for h in range(heads):
+        cols = slice(h * HEAD, (h + 1) * HEAD)
+        back = back_state[h * per_head : (h + 1) * per_head].reshape(HEAD, HEAD)
+        fade = shrink[:, h : h + 1]
+        for i, (part, other, over, out, out_hbm) in enumerate(
+            ((dk_part, v, 1, dk, dk_hbm), (dv_part, k, 0, dv, dv_hbm))
+        ):
+            out[:, cols] = (part[:, cols] + fade * dot(other[:, cols], back, 1, over)).astype(BF16)
+            copies.append(pltpu.make_async_copy(out.at[:, cols], out_hbm.at[:, cols], sem.at[3 + 2 * h + i]))
+            copies[-1].start()
     for copy in copies:
         copy.wait()
 
@@ -376,16 +389,22 @@
     ]
     outs = pl.pallas_call(
         functools.partial(kernel, n, m, heads),
-        out_shape=[jax.ShapeDtypeStruct(square, BF16)] * 4 + [jax.ShapeDtypeStruct((heads, HEAD), F32)],
+        out_shape=[
+            jax.ShapeDtypeStruct(shape, kind)
+            for shape, kind in (
+                (square, BF16), (square, BF16), ((heads, HEAD), F32), (square, BF16), (square, BF16),
+                ((BLOCK, 16), F32), ((n, *piece), BF16), (square, F32), (square, F32),
+            )
+        ],
         in_specs=[pl.BlockSpec(memory_space=pltpu.HBM)] * 7,
-        out_specs=[pl.BlockSpec(memory_space=pltpu.VMEM)] * 5,
+        out_specs=[pl.BlockSpec(memory_space=pltpu.VMEM)] * 9,
         scratch_shapes=[
             vmem((heads, BLOCK), F32), vmem((heads, HEAD), F32),
-            *[vmem(square, BF16)] * 5,
+            *[vmem(square, BF16)] * 3,
             vmem((16, BLOCK), F32), vmem((BLOCK, BLOCK), BF16),
-            vmem((BLOCK, 16), F32), vmem((16, BLOCK), F32), vmem((BLOCK, 16), F32), vmem((BLOCK, 16), F32),
+            vmem((BLOCK, 16), F32), vmem((16, BLOCK), F32), vmem((BLOCK, 16), F32),
             vmem(pairs, F32), vmem(pairs, BF16), vmem(pairs, BF16),
-            *[vmem(square, F32)] * 3, vmem(square, BF16), *[vmem((width, BLOCK), BF16)] * 2, *[vmem(square, F32)] * 2,
+            *[vmem(square, F32)] * 3, vmem(square, BF16), *[vmem((width, BLOCK), BF16)] * 2,
             *[vmem((heads, 1, HEAD), F32)] * 3, vmem((n // 2, 1, HEAD), F32),
             vmem((2 * CHUNKS, CHUNK), F32), vmem((m, 2 * CHUNKS, CHUNK), F32),
             vmem((CHUNK, CHUNK), F32), vmem((CHUNK, CHUNK), F32),
@@ -396,15 +415,16 @@
             pltpu.SemaphoreType.DMA((SEMAPHORES,)), pltpu.SemaphoreType.DMA((SEMAPHORES,)),
         ],
         compiler_params=pltpu.CompilerParams(
-            collective_id=0, has_side_effects=True, vmem_limit_bytes=48 << 20
+            collective_id=0, has_side_effects=True, vmem_limit_bytes=40 << 20
         ),
     )(*[pltpu.with_memory_space_constraint(x, pltpu.HBM) for x in (log_decay, gain.reshape(heads, HEAD), keys, values, queries, gate, grad_out)])
-    dq, dk, dv, dgate, dgain = pl.pallas_call(
-        put,
-        out_shape=[jax.ShapeDtypeStruct(x.shape, x.dtype) for x in outs],
-        in_specs=[pl.BlockSpec(memory_space=pl.ANY)] * len(outs),
-        out_specs=[pl.BlockSpec(memory_space=pltpu.HBM)] * len(outs),
-        scratch_shapes=[pltpu.SemaphoreType.DMA((len(outs),))],
+    dq, dgate, dgain, dk, dv = pl.pallas_call(
+        finish,
+        out_shape=[jax.ShapeDtypeStruct(x.shape, x.dtype) for x in (*outs[:3], *outs[:2])],
+        in_specs=[pl.BlockSpec(memory_space=pltpu.VMEM)] * len(outs),
+        out_specs=[pl.BlockSpec(memory_space=pltpu.HBM)] * 5,
+        scratch_shapes=[*[vmem(square, BF16)] * 2, pltpu.SemaphoreType.DMA((3 + 2 * heads,))],
+        compiler_params=pltpu.CompilerParams(vmem_limit_bytes=16 << 20),
     )(*[pltpu.with_memory_space_constraint(x, pltpu.VMEM) for x in outs])
     return dq, dk, dv, dgate, dgain.reshape(width)
 

time: 47.1 us -> 46.1 us (0.979)
  Pallas kernels: 46.4 us -> 45.3 us
    pallas_call x1, Pallas kernels: 45 us -> 43.9 us  [local(): pl.pallas_call(functools.partial(kernel, n, m, heads), out_shape=[jax.Sha...]
where the time goes in v3:
time: 46.1 us; the launch traced here: 45.9 us
  Pallas kernels  45.3 us (98%)
  between operations  0.64 us (1%)
    pallas_call x1, Pallas kernels, local(): pl.pallas_call(functools.partial(kernel, n, m, heads), out_shape=[jax.Sha...  43.9 us
    pallas_call x1, Pallas kernels, local(): pl.pallas_call(finish, out_shape=[jax.ShapeDtypeStruct(x.shape, x.dtype)...  1.4 us

profile of v3, /device:TPU:1, one launch (start us, length us, event | category | flops | bytes accessed | tf_op | source)
XLA Modules:
  0.0 45.9 jit_solution(9145574874251325369)
XLA Ops:
  0.6 43.9 %shard_map.110 = (bf16[512,512]{1,0:T(8,128)(2,1)S(1)}, bf16[512,512]{1,0:T(8,128)(2,1)S(1)}, f32[4,128]{1,0:T(4,128)S(1)}, bf16[512,512]{1,0:T(8,128)(2,1)S(1)}...) custom-call(f32[4,512]{1,0:T(4,128)} %ld_hbm.1, ...), custom_call_target="tpu_custom_call" | custom-call | tf_op jit(solution)/shard_map/pallas_call | solution.py:390
  44.5 1.4 %shard_map.111 = (bf16[512,512]{1,0:T(8,128)(2,1)}, bf16[512,512]{1,0:T(8,128)(2,1)}, f32[4,128]{1,0:T(4,128)}, bf16[512,512]{1,0:T(8,128)(2,1)}, bf16[512,512]{1,0:T(8,128)(2,1)}) custom-call(bf16[512,512]{1,0:T(8,128)(2,1)S(1)} %get-tuple-element.19.dq, bf16[512,512]{1,0:T(8,128)(2,1)S(1)} %get-tuple-element.20.dgate, ...), custom_call_target="tpu_custom_call" | custom-call | tf_op jit(solution)/shard_map/pallas_call | solution.py:421

commit v4 on v3

--- a/solution.py
+++ b/solution.py
@@ -15,9 +15,9 @@
 MESH = pl.DeviceIdType.MESH
 F32, BF16 = jnp.float32, jnp.bfloat16
 
-DECAY_PAIR, DECAY, GRAD, NORM, GAIN_PAIR, GAIN, FORWARD, BACKWARD = 0, 1, 2, 3, 4, 5, 6, 11
-URGENT, REST, UP, DOWN, WHOLE = range(5)
-SEMAPHORES = 16
+DECAY_PAIR, DECAY, GRAD, NORM, GAIN_PAIR, GAIN, FORWARD, BACKWARD = 0, 1, 2, 3, 4, 5, 6, 10
+URGENT, REST, UP, DOWN = range(4)
+SEMAPHORES = 14
 
 
 def dot(a, b, over_a, over_b):
@@ -41,7 +41,7 @@
     dq, dgate, dgain, k, v, shrink, back_state, dk_part, dv_part,
     ld, gain, q, gate, grad,
     ld_rows, tri, cum_col, cum_row, grow,
-    table, probs, dscores, attention, dnorm, closed, dattn, q_high, q_low,
+    table, probs, dscores, attention, dnorm, dscaled, closed, dattn, q_both,
     decay_own, decay_pair, decay_out, decay_in,
     norm_out, norm_in, coefs, columns, gain_own, gain_pair, gain_in,
     fore_own, fore_out, fore_pair, fore_up_out, fore_up_in, fore_down, fore_whole, fore_state,
@@ -51,12 +51,13 @@
     me, mt = lax.axis_index("ctx"), lax.axis_index("tp")
     core, chip = lax.rem(me, 2), me // 2
     chips, deep = n // 2, n // 4
-    per_head = n // heads
+    slices = chips // 2
+    per_head = 2 * slices // heads
     channels = heads * HEAD * m
     width = heads * HEAD
     grad_rows = BLOCK // m
-    half = pl.ds(core * chips, chips)
-    other_half = pl.ds((1 - core) * chips, chips)
+    half = pl.ds(core * slices, slices)
+    other_half = pl.ds((1 - core) * slices, slices)
 
     loads = [
         pltpu.make_async_copy(src, dst, in_sem.at[i])
@@ -67,12 +68,13 @@
     for load in loads:
         load.start()
 
-    peers = [
-        lax.rem(chip // deep + y, 2) * deep + lax.rem(chip + z, deep)
-        for z in far_first(deep)
-        for y in (1, 0)
-        if (y, z) != (0, 0)
-    ]
+    def chip_at(y, z):
+        return lax.rem(chip // deep + y, 2) * deep + lax.rem(chip + z + deep, deep)
+
+    peers = [chip_at(y, z) for z in far_first(deep) for y in (1, 0) if (y, z) != (0, 0)]
+    near = sorted(range(1 - deep // 4, deep // 4 + 1), key=lambda z: -abs(z))
+    served = [(y, z, c) for z in near for y in (1, 0) for c in (0, 1) if (y, z, c) != (0, 0, 0)]
+    across = [(y, z) for z in range(-(deep // 4), deep // 4 + 1) for y in (1, 0) if (y, z) != (0, 0)]
     tp_peers = [
         lax.rem(mt // 2 + x, m // 2) * 2 + lax.rem(mt + y, 2)
         for y in (1, 0)
@@ -90,6 +92,7 @@
 
     barrier = pltpu.get_barrier_semaphore()
     greeted = [on_chip(p) for p in peers] + [on_tp(p) for p in tp_peers] + [sibling]
+    greeted += [{"ctx": 2 * chip_at(y, z) + 1 - core, "tp": mt} for y, z in across]
     for device in greeted:
         pl.semaphore_signal(barrier, inc=1, device_id=device, device_id_type=MESH)
 
@@ -120,6 +123,11 @@
 
     def state(ref, h):
         return ref[pieces(h)].reshape(HEAD, HEAD)
+
+    def slice_of(p):
+        return (p // deep) * (deep // 2) + lax.rem(p, deep // 2)
+
+    mine = core * slices + slice_of(chip)
 
     t = lax.broadcasted_iota(jnp.int32, (BLOCK, BLOCK), 0)
     u = lax.broadcasted_iota(jnp.int32, (BLOCK, BLOCK), 1)
@@ -154,13 +162,13 @@
         arrived(pair.at[half], first + URGENT)
         for g in range(heads // 2):
             h = core * (heads // 2) + g
-            here = pl.ds(core * chips + g * per_head, per_head)
+            here = pl.ds(core * slices + g * per_head, per_head)
             by_own = leads * decay_pair[h] + (1.0 - leads)
             by_pair = leads + (1.0 - leads) * decay_own[h]
             up_out[pieces(g)] = (own[here] * by_own + pair[here].astype(F32) * by_pair).astype(BF16)
         for p in peers:
-            send(up_out.at[p], up_in.at[chip], first + UP, on_chip(p))
-        up_in[chip] = up_out[chip]
+            send(up_out.at[slice_of(p)], up_in.at[chip], first + UP, on_chip(p))
+        up_in[chip] = up_out[slice_of(chip)]
 
     def scan(up_in, down, whole, order, first):
         arrived(up_in.at[pl.ds(0, chips - 1)], first + UP)
@@ -168,15 +176,14 @@
         for j in order:
             down[j] = carried.astype(BF16)
             carried = carried * decay_in[j] + up_in[j].astype(F32)
-        for p in peers:
-            send(down.at[p], whole.at[core * chips + chip], first + DOWN, on_chip(p))
-        whole[core * chips + chip] = down[chip]
+        for y, z, c in served:
+            p = chip_at(y, z * (1 - 2 * core))
+            send(down.at[p], whole.at[mine], first + DOWN, {"ctx": 2 * p + lax.rem(core + c, 2), "tp": mt})
+        whole[mine] = down[chip]
 
     def settle(whole, pair, first):
-        arrived(whole.at[pl.ds(0, chips - 1)], first + DOWN)
-        send(whole.at[half], whole.at[half], first + WHOLE, sibling)
         arrived(pair.at[other_half], first + REST)
-        arrived(whole.at[other_half], first + WHOLE)
+        arrived(whole.at[pl.ds(0, len(served))], first + DOWN)
 
     def entering(whole, pair, leads, h):
         by_chip = leads + (1.0 - leads) * decay_pair[h]
@@ -207,8 +214,8 @@
     arrived(decay_pair, DECAY_PAIR)
     decay_out[...] = decay_own[...] * decay_pair[...]
     for p in peers:
-        send(decay_out.at[(core * chips + p) // per_head], decay_in.at[chip], DECAY, on_chip(p))
-    decay_in[chip] = decay_out[(core * chips + chip) // per_head]
+        send(decay_out.at[(core * slices + slice_of(p)) // per_head], decay_in.at[chip], DECAY, on_chip(p))
+    decay_in[chip] = decay_out[mine // per_head]
     join(fore_own, fore_pair, fore_up_out, fore_up_in, fore_leads, FORWARD)
 
     cum_row[...] = dot(part0, tri[...], 1, 1) + dot(part1, tri[...], 1, 1) + dot(part2, tri[...], 1, 1)
@@ -230,8 +237,8 @@
             probs[h, rows(r), 0:w] = p
             attention[rows(r), cols(h)] = dot(p, v[0:w, cols(h)], 1, 0)
         high, low = halves(q[:, cols(h)].astype(F32) * grow[:, h : h + 1])
-        q_high[cols(h), :] = jnp.transpose(high)
-        q_low[cols(h), :] = jnp.transpose(low)
+        q_both[h, 0:HEAD, :] = jnp.transpose(high)
+        q_both[h, HEAD : 2 * HEAD, :] = jnp.transpose(low)
 
     for h in range(heads // 2):
         inside(h)
@@ -249,27 +256,31 @@
     for r in range(CHUNKS):
         for h in range(heads):
             opened = jax.nn.sigmoid(gate[rows(r), cols(h)].astype(F32))
-            dnorm[rows(r), cols(h)] = grad[rows(r), cols(h)].astype(F32) * opened
+            d = grad[rows(r), cols(h)].astype(F32) * opened
+            dnorm[rows(r), cols(h)] = d
+            dscaled[rows(r), cols(h)] = d * gain[h : h + 1, :]
             closed[rows(r), cols(h)] = 1.0 - opened
 
     settle(fore_whole, fore_pair, FORWARD)
     for h in range(heads):
         fore_state[pieces(h)] = entering(fore_whole, fore_pair, fore_leads, h)
     ones = jnp.ones((16, HEAD), BF16)
-    for r in range(CHUNKS):
-        squares = jnp.zeros((CHUNK, HEAD), F32)
-        inner = jnp.zeros((CHUNK, HEAD), F32)
+    for b in range(CHUNKS // 2):
+        two = slice(2 * b * CHUNK, 2 * (b + 1) * CHUNK)
+        squares = jnp.zeros((2 * CHUNK, HEAD), F32)
+        inner = jnp.zeros((2 * CHUNK, HEAD), F32)
         for h in range(heads):
-            a = attention[rows(r), cols(h)] + grow[rows(r), h : h + 1] * dot(
-                q[rows(r), cols(h)], state(fore_state, h), 1, 0
+            a = attention[two, cols(h)] + grow[two, h : h + 1] * dot(
+                q[two, cols(h)], state(fore_state, h), 1, 0
             )
-            attention[rows(r), cols(h)] = a
+            attention[two, cols(h)] = a
             squares = squares + a * a
-            inner = inner + a * (dnorm[rows(r), cols(h)] * gain[h : h + 1, :])
-        for place, total in ((r, squares), (CHUNKS + r, inner)):
+            inner = inner + a * dscaled[two, cols(h)]
+        for place, total in ((2 * b, squares), (CHUNKS + 2 * b, inner)):
             high, low = halves(total)
             line = dot(ones, high, 1, 1) + dot(ones, low, 1, 1)
-            norm_out[place : place + 1, :] = line[0:1, :]
+            norm_out[place : place + 1, :] = line[0:1, 0:CHUNK]
+            norm_out[place + 1 : place + 2, :] = line[0:1, CHUNK : 2 * CHUNK]
     for p in tp_peers:
         send(norm_out, norm_in.at[mt], NORM, on_tp(p))
     norm_in[mt] = norm_out[...]
@@ -285,10 +296,11 @@
     for r in range(CHUNKS):
         scale, pull = columns[:, r : r + 1], columns[:, CHUNKS + r : CHUNKS + r + 1]
         for h in range(heads):
-            d = dnorm[rows(r), cols(h)] * gain[h : h + 1, :] * scale - attention[rows(r), cols(h)] * pull
+            d = dscaled[rows(r), cols(h)] * scale - attention[rows(r), cols(h)] * pull
             dattn[rows(r), cols(h)] = d.astype(BF16)
     for h in range(heads):
-        share(h, dot(q_high[cols(h), :], dattn[:, cols(h)], 1, 0) + dot(q_low[cols(h), :], dattn[:, cols(h)], 1, 0), back_own, back_out)
+        both = dot(q_both[h], dattn[:, cols(h)], 1, 0)
+        share(h, both[0:HEAD] + both[HEAD : 2 * HEAD], back_own, back_out)
     swap(back_out, back_pair, BACKWARD)
 
     for h in range(heads):
@@ -342,10 +354,14 @@
     sent(norm_in.at[pl.ds(0, m - 1)], NORM)
     sent(gain_own, GAIN_PAIR)
     sent(gain_in.at[pl.ds(0, chips - 1)], GAIN)
-    for first, up_out in ((FORWARD, fore_up_out), (BACKWARD, back_up_out)):
-        one_less = up_out.at[pl.ds(0, chips - 1)]
-        for which, some in ((URGENT, up_out), (REST, up_out), (UP, one_less), (DOWN, one_less), (WHOLE, up_out)):
-            sent(some, first + which)
+    for first, up_out, up_in, whole in (
+        (FORWARD, fore_up_out, fore_up_in, fore_whole),
+        (BACKWARD, back_up_out, back_up_in, back_whole),
+    ):
+        sent(up_out, first + URGENT)
+        sent(up_out, first + REST)
+        sent(up_in.at[pl.ds(0, chips - 1)], first + UP)
+        sent(whole.at[pl.ds(0, len(served))], first + DOWN)
 
 
 def finish(
@@ -378,14 +394,15 @@
 def local(n, m, queries, keys, values, log_decay, gate, gain, grad_out):
     heads = queries.shape[1] // HEAD
     width = heads * HEAD
-    assert queries.shape[0] == BLOCK and n % heads == 0
-    piece = (heads * HEAD // n, HEAD)
+    assert queries.shape[0] == BLOCK and n % (2 * heads) == 0
+    count = n // 2
+    piece = (width // count, HEAD)
     square = (BLOCK, width)
     pairs = (heads, BLOCK, BLOCK)
     vmem = pltpu.VMEM
     sweep = [
-        vmem((n, *piece), F32), *[vmem((n, *piece), BF16)] * 2,
-        *[vmem((n // 2, *piece), BF16)] * 3, vmem((n, *piece), BF16),
+        vmem((count, *piece), F32), *[vmem((count, *piece), BF16)] * 2,
+        vmem((count // 2, *piece), BF16), *[vmem((n // 2, *piece), BF16)] * 2, vmem((count, *piece), BF16),
     ]
     outs = pl.pallas_call(
         functools.partial(kernel, n, m, heads),
@@ -393,7 +410,7 @@
             jax.ShapeDtypeStruct(shape, kind)
             for shape, kind in (
                 (square, BF16), (square, BF16), ((heads, HEAD), F32), (square, BF16), (square, BF16),
-                ((BLOCK, 16), F32), ((n, *piece), BF16), (square, F32), (square, F32),
+                ((BLOCK, 16), F32), ((count, *piece), BF16), (square, F32), (square, F32),
             )
         ],
         in_specs=[pl.BlockSpec(memory_space=pltpu.HBM)] * 7,
@@ -404,12 +421,12 @@
             vmem((16, BLOCK), F32), vmem((BLOCK, BLOCK), BF16),
             vmem((BLOCK, 16), F32), vmem((16, BLOCK), F32), vmem((BLOCK, 16), F32),
             vmem(pairs, F32), vmem(pairs, BF16), vmem(pairs, BF16),
-            *[vmem(square, F32)] * 3, vmem(square, BF16), *[vmem((width, BLOCK), BF16)] * 2,
+            *[vmem(square, F32)] * 4, vmem(square, BF16), vmem((heads, 2 * HEAD, BLOCK), BF16),
             *[vmem((heads, 1, HEAD), F32)] * 3, vmem((n // 2, 1, HEAD), F32),
             vmem((2 * CHUNKS, CHUNK), F32), vmem((m, 2 * CHUNKS, CHUNK), F32),
             vmem((CHUNK, CHUNK), F32), vmem((CHUNK, CHUNK), F32),
             *[vmem((heads, HEAD), F32)] * 2, vmem((n // 2, heads, HEAD), F32),
-            *sweep, vmem((n, *piece), BF16),
+            *sweep, vmem((count, *piece), BF16),
             *sweep,
             pltpu.SemaphoreType.DMA((7,)),
             pltpu.SemaphoreType.DMA((SEMAPHORES,)), pltpu.SemaphoreType.DMA((SEMAPHORES,)),

time: 46.1 us -> 45 us (0.976)
  Pallas kernels: 45.3 us -> 44.2 us
    pallas_call x1, Pallas kernels: 43.9 us -> 42.8 us  [local(): pl.pallas_call(functools.partial(kernel, n, m, heads), out_shape=[jax.Sha...]
where the time goes in v4:
time: 45 us; the launch traced here: 44.8 us
  Pallas kernels  44.2 us (98%)
  between operations  0.64 us (1%)
    pallas_call x1, Pallas kernels, local(): pl.pallas_call(functools.partial(kernel, n, m, heads), out_shape=[jax.Sha...  42.8 us
    pallas_call x1, Pallas kernels, local(): pl.pallas_call(finish, out_shape=[jax.ShapeDtypeStruct(x.shape, x.dtype)...  1.4 us

profile of v4, /device:TPU:1, one launch (start us, length us, event | category | flops | bytes accessed | tf_op | source)
XLA Modules:
  0.0 44.8 jit_solution(6465086130204095377)
XLA Ops:
  0.6 42.8 %shard_map.110 = (bf16[512,512]{1,0:T(8,128)(2,1)S(1)}, bf16[512,512]{1,0:T(8,128)(2,1)S(1)}, f32[4,128]{1,0:T(4,128)S(1)}, bf16[512,512]{1,0:T(8,128)(2,1)S(1)}...) custom-call(f32[4,512]{1,0:T(4,128)} %ld_hbm.1, ...), custom_call_target="tpu_custom_call" | custom-call | tf_op jit(solution)/shard_map/pallas_call | solution.py:407
  43.4 1.4 %shard_map.111 = (bf16[512,512]{1,0:T(8,128)(2,1)}, bf16[512,512]{1,0:T(8,128)(2,1)}, f32[4,128]{1,0:T(4,128)}, bf16[512,512]{1,0:T(8,128)(2,1)}, bf16[512,512]{1,0:T(8,128)(2,1)}) custom-call(bf16[512,512]{1,0:T(8,128)(2,1)S(1)} %get-tuple-element.19.dq, bf16[512,512]{1,0:T(8,128)(2,1)S(1)} %get-tuple-element.20.dgate, ...), custom_call_target="tpu_custom_call" | custom-call | tf_op jit(solution)/shard_map/pallas_call | solution.py:438

commit v5 on v4

--- a/solution.py
+++ b/solution.py
@@ -202,21 +202,22 @@
     send(decay_own, decay_pair, DECAY_PAIR, sibling)
     swap(fore_out, fore_pair, FORWARD)
 
-    def grad_part(p):
-        return grad_hbm.at[:, pl.ds(pl.multiple_of(p * width, width), width)]
-
-    grad_place = grad.at[pl.ds(pl.multiple_of(mt * grad_rows, grad_rows), grad_rows), :]
-    own_grad = pltpu.make_async_copy(grad_part(mt), grad_place, in_sem.at[6])
-    own_grad.start()
-    for p in tp_peers:
-        send(grad_part(p), grad_place, GRAD, on_tp(p))
-
     arrived(decay_pair, DECAY_PAIR)
     decay_out[...] = decay_own[...] * decay_pair[...]
     for p in peers:
         send(decay_out.at[(core * slices + slice_of(p)) // per_head], decay_in.at[chip], DECAY, on_chip(p))
     decay_in[chip] = decay_out[mine // per_head]
     join(fore_own, fore_pair, fore_up_out, fore_up_in, fore_leads, FORWARD)
+
+    def grad_part(p):
+        return grad_hbm.at[:, pl.ds(pl.multiple_of(p * width, width), width)]
+
+    grad_place = grad.at[pl.ds(pl.multiple_of(mt * grad_rows, grad_rows), grad_rows), :]
+    own_grad = pltpu.make_async_copy(grad_part(mt), grad_place, in_sem.at[6])
+    own_grad.start()
+    for p in tp_peers:
+        send(grad_part(p), grad_place, GRAD, on_tp(p))
+
 
     cum_row[...] = dot(part0, tri[...], 1, 1) + dot(part1, tri[...], 1, 1) + dot(part2, tri[...], 1, 1)
     loads[3].wait()

time: 45 us -> 45.1 us (level)
  no operation moved by 1% of the time
where the time goes in v5:
time: 45.1 us; the launch traced here: 45 us
  Pallas kernels  44.3 us (98%)
  between operations  0.64 us (1%)
    pallas_call x1, Pallas kernels, local(): pl.pallas_call(functools.partial(kernel, n, m, heads), out_shape=[jax.Sha...  42.9 us
    pallas_call x1, Pallas kernels, local(): pl.pallas_call(finish, out_shape=[jax.ShapeDtypeStruct(x.shape, x.dtype)...  1.4 us

profile of v5, /device:TPU:1, one launch (start us, length us, event | category | flops | bytes accessed | tf_op | source)
XLA Modules:
  0.0 45.0 jit_solution(1814709614421804328)
XLA Ops:
  0.6 42.9 %shard_map.110 = (bf16[512,512]{1,0:T(8,128)(2,1)S(1)}, bf16[512,512]{1,0:T(8,128)(2,1)S(1)}, f32[4,128]{1,0:T(4,128)S(1)}, bf16[512,512]{1,0:T(8,128)(2,1)S(1)}...) custom-call(f32[4,512]{1,0:T(4,128)} %ld_hbm.1, ...), custom_call_target="tpu_custom_call" | custom-call | tf_op jit(solution)/shard_map/pallas_call | solution.py:408
  43.6 1.4 %shard_map.111 = (bf16[512,512]{1,0:T(8,128)(2,1)}, bf16[512,512]{1,0:T(8,128)(2,1)}, f32[4,128]{1,0:T(4,128)}, bf16[512,512]{1,0:T(8,128)(2,1)}, bf16[512,512]{1,0:T(8,128)(2,1)}) custom-call(bf16[512,512]{1,0:T(8,128)(2,1)S(1)} %get-tuple-element.19.dq, bf16[512,512]{1,0:T(8,128)(2,1)S(1)} %get-tuple-element.20.dgate, ...), custom_call_target="tpu_custom_call" | custom-call | tf_op jit(solution)/shard_map/pallas_call | solution.py:439
